TPU v7x, 32 devices: a whole 2x2x4 slice. The times are simulated.
32 devices in a mesh: seq: 8 (over z, x), head: 4 (over y, core).
Axes of the slice: x: 2, y: 2, z: 4, core: 2. Of those that a mesh axis runs over, the one named last changes fastest.
Arguments:
- tokens: bfloat16 [2, 2048, 1024], P(None, 'seq', 'head'), may hold values from -6 to 6
- cotangent: bfloat16 [2, 2048, 1024], P(None, 'seq', 'head'), may hold values from -6 to 6
- w_qkv: bfloat16 [1024, 3, 1024], P('seq', None, 'head'), may hold values from -0.1875 to 0.1875
- w_out_t: bfloat16 [1024, 1024], P('seq', 'head'), may hold values from -0.75 to 0.75
- w_up: bfloat16 [1024, 4096], P('seq', 'head'), may hold values from -0.1875 to 0.1875
- w_down_t: bfloat16 [1024, 4096], P('seq', 'head'), may hold values from -0.09375 to 0.09375
- gains: bfloat16 [2, 1024], P(None, 'seq'), may hold values from 0.099609375 to 1.8984375
- biases: bfloat16 [3, 1024], P(None, 'seq'), may hold values from -3 to 3
- up_bias: bfloat16 [4, 1024], P('head', 'seq'), may hold values from -3 to 3
- lengths: int32 [2, 16], replicated, may hold values from 1 to 512, 2048 in all within a row
- pixel_mask: int32 [2, 2048], P(None, 'seq'), may hold values 0 or 1
Outputs:
- activations: float32 [2, 2048, 1024], P(None, 'seq', 'head')
- input_grad: float32 [2, 2048, 1024], P(None, 'seq', 'head')
- grad_qkv: float32 [1024, 3, 1024], P('seq', None, 'head')
- grad_out_t: float32 [1024, 1024], P('seq', 'head')
- grad_up: float32 [1024, 4096], P('seq', 'head')
- grad_down_t: float32 [1024, 4096], P('seq', 'head')
- grad_gains: float32 [2, 1024], P(None, 'seq')
- grad_biases: float32 [3, 1024], P(None, 'seq')
- grad_up_bias: float32 [4, 1024], P('head', 'seq')
Inputs may be any that keep to these rules, and one draw needn't show every extreme that they name: `lengths`: row b lists the 16 crops of micro-batch b in order of their place; each row sums to 2048 and its longest crop has 512 tokens.
All inputs are finite; a program needn't handle non-finite values. No bound on the sum of `pixel_mask` on one device may be relied on, other than what follows from the above.
Results may differ from a plain program's by a relative error of at most 0.017.
Values may be sent and summed in bfloat16 or wider, within the bound.
A program may use at most 128 MiB of HBM per device.

v0:
```python
import jax
import jax.numpy as jnp
from jax import lax
from jax.sharding import PartitionSpec as P

DH = 64


highest = lax.Precision.HIGHEST
epsilon = 1e-05


def entering(array, axis, join, neutral):
    place = lax.axis_index(axis)
    gathered = jax.tree.map(
        lambda a, kind: lax.all_gather(a.astype(kind), axis),
        array,
        (jnp.bfloat16, jnp.bfloat16, jnp.bfloat16),
    )
    state = jax.tree.map(lambda a, e: jnp.zeros_like(a) + jnp.asarray(e, a.dtype), array, neutral)

    def one(hop, state):
        return join(
            state,
            jax.tree.map(
                lambda a, own: lax.dynamic_index_in_dim(a, hop, 0, False).astype(own.dtype),
                gathered,
                array,
            ),
        )

    return lax.fori_loop(0, place, one, state)


def entering_2(array, axis, combine, identity):
    length, place = (lax.axis_size(axis), lax.axis_index(axis))
    everything = jax.tree.map(
        lambda part, kind: lax.all_gather(part.astype(kind), axis),
        array,
        jax.tree.map(lambda a: jnp.bfloat16 if a.dtype == jnp.float32 else a.dtype, array),
    )
    start = jax.tree.map(
        lambda part, zero: jnp.broadcast_to(jnp.asarray(zero, part.dtype), part.shape),
        array,
        identity,
    )

    def hop(k, before):
        at = length - 1 - k
        reached = at > place
        new = combine(
            before, jax.tree.map(lambda part, own: part[at].astype(own.dtype), everything, array)
        )
        return jax.tree.map(lambda a, b: jnp.where(reached, a, b), new, before)

    return lax.fori_loop(0, length, hop, start)


def normalize(values, gain_vec, shift_vec):
    mean_val = jnp.mean(values, axis=-1, keepdims=True)
    centered = values - mean_val
    inverse = lax.rsqrt(jnp.mean(centered * centered, axis=-1, keepdims=True) + epsilon)
    unit_val = centered * inverse
    return (unit_val * gain_vec + shift_vec, unit_val, inverse)


def norm_back(grad_in, unit_val, inverse, gain_vec):
    scaled = grad_in * gain_vec
    centered = scaled - jnp.mean(scaled, axis=-1, keepdims=True)
    return inverse * (centered - unit_val * jnp.mean(scaled * unit_val, axis=-1, keepdims=True))


def features(values):
    return jax.nn.elu(values) + 1.0


def finish(numerator, denominator):
    return numerator / jnp.maximum(denominator, 1.0)[:, :, None]


def compose(earlier, later):
    return (
        later[0] + later[2] * earlier[0],
        later[1] + later[2] * earlier[1],
        later[2] * earlier[2],
    )


def item_numbers(lengths_row, first_place, number):
    offsets = jnp.cumsum(lengths_row) - lengths_row
    places = first_place + jnp.arange(number, dtype=jnp.int32)
    return jnp.sum((offsets[None, :] <= places[:, None]).astype(jnp.int32), axis=1) - 1


def on_device(
    tokens, cotangent, w_qkv, w_out_t, w_up, w_down_t, gains, biases, up_bias, lengths, pixel_mask
):
    batches, local_rows, columns = tokens.shape
    local_width = w_qkv.shape[2]
    heads_here = local_width // DH
    seq_index = lax.axis_index("seq")
    head_index = lax.axis_index("head")
    first_token = seq_index * local_rows
    position = jnp.arange(local_rows, dtype=jnp.int32)
    before = position[:, None] >= position[None, :]

    def own_columns(matrix):
        return lax.dynamic_slice_in_dim(matrix, head_index * columns, columns, 1)

    results = []
    input_grads = []
    shard_sums = None
    for batch_index in range(batches):
        full_qkv, full_out, full_up, full_down, full_gains, full_biases, full_upb = (
            lax.all_gather(w_qkv, "seq", axis=0, tiled=True),
            lax.all_gather(w_out_t, "seq", axis=0, tiled=True),
            lax.all_gather(w_up, "seq", axis=0, tiled=True),
            lax.all_gather(w_down_t, "seq", axis=0, tiled=True),
            lax.all_gather(gains, "seq", axis=1, tiled=True),
            lax.all_gather(biases, "seq", axis=1, tiled=True),
            lax.all_gather(up_bias, "seq", axis=1, tiled=True),
        )
        input_rows, grad_rows16 = (
            lax.all_gather(tokens[batch_index], "head", axis=1, tiled=True),
            lax.all_gather(cotangent[batch_index], "head", axis=1, tiled=True),
        )
        gains32 = full_gains.astype(jnp.float32)
        biases32 = full_biases.astype(jnp.float32)
        upb32 = full_upb.astype(jnp.float32).reshape(-1)
        inputs32 = input_rows.astype(jnp.float32)
        place_items = item_numbers(lengths[batch_index], first_token - 1, local_rows + 1)
        item_of = place_items[1:]
        carried = (item_of == place_items[0]).astype(jnp.float32)
        tail_mask = (item_of == item_of[local_rows - 1]).astype(jnp.float32)
        through = carried[local_rows - 1]
        same_item = ((item_of[:, None] == item_of[None, :]) & before).astype(jnp.float32)
        keep_half = pixel_mask[batch_index].astype(jnp.bfloat16)
        keep32 = pixel_mask[batch_index].astype(jnp.float32)
        lifted, unit_one, inverse_one = normalize(inputs32, gains32[0], biases32[0])
        normed = lifted.astype(jnp.bfloat16)
        projected = jnp.einsum("td,dsf->tsf", normed, full_qkv, preferred_element_type=jnp.float32)
        query_feat = (
            features(projected[:, 0]).astype(jnp.bfloat16).reshape(local_rows, heads_here, DH)
        )
        key_feat = (features(projected[:, 1]).astype(jnp.bfloat16) * keep_half[:, None]).reshape(
            local_rows, heads_here, DH
        )
        value_feat = projected[:, 2].astype(jnp.bfloat16).reshape(local_rows, heads_here, DH)
        tail_key = key_feat * tail_mask.astype(jnp.bfloat16)[:, None, None]
        state_loc = jnp.einsum(
            "jhd,jhe->hde", tail_key, value_feat, preferred_element_type=jnp.float32
        )
        total_loc = jnp.sum(tail_key.astype(jnp.float32), axis=0)
        identity = (jnp.zeros_like(state_loc), jnp.zeros_like(total_loc), jnp.ones((), jnp.float32))
        state_in, total_in, passed = entering(
            (state_loc, total_loc, through), "seq", compose, identity
        )
        query32 = query_feat.astype(jnp.float32)
        scores = (
            jnp.einsum("thd,jhd->htj", query_feat, key_feat, preferred_element_type=jnp.float32)
            * same_item[None]
        )
        scores_low = scores.astype(jnp.bfloat16)
        numerator = jnp.einsum(
            "htj,jhe->the", scores_low, value_feat, preferred_element_type=jnp.float32
        ) + carried[:, None, None] * jnp.einsum(
            "thd,hde->the", query32, state_in, precision=highest
        )
        denominator = jnp.sum(scores, axis=2).T + carried[:, None] * jnp.einsum(
            "thd,hd->th", query32, total_in, precision=highest
        )
        output, finish_back = jax.vjp(finish, numerator, denominator)
        mixed_out = output.reshape(local_rows, local_width).astype(jnp.bfloat16)
        attended = lax.psum(
            jnp.einsum("tf,df->td", mixed_out, full_out, preferred_element_type=jnp.float32).astype(
                jnp.bfloat16
            ),
            "head",
        ).astype(jnp.float32)
        middle = inputs32 + attended
        lifted_two, unit_two, inverse_two = normalize(middle, gains32[1], biases32[1])
        normed_two = lifted_two.astype(jnp.bfloat16)
        hidden = jnp.dot(normed_two, full_up, preferred_element_type=jnp.float32) + upb32
        activated32, gelu_back = jax.vjp(jax.nn.gelu, hidden)
        activated = activated32.astype(jnp.bfloat16)
        branch = lax.psum_scatter(
            jnp.einsum(
                "tf,df->td", activated, full_down, preferred_element_type=jnp.float32
            ).astype(jnp.bfloat16),
            "head",
            scatter_dimension=1,
            tiled=True,
        ).astype(jnp.float32)
        results.append(own_columns(middle) + branch + own_columns(biases32[2][None]))
        grad_out = grad_rows16.astype(jnp.float32)
        grad_down = jnp.einsum(
            "td,tf->df", grad_rows16, activated, preferred_element_type=jnp.float32
        )
        grad_act = jnp.einsum(
            "td,df->tf", grad_rows16, full_down, preferred_element_type=jnp.float32
        )
        grad_hidden = gelu_back(grad_act)[0].astype(jnp.bfloat16)
        grad_up = jnp.einsum(
            "td,tf->df", normed_two, grad_hidden, preferred_element_type=jnp.float32
        )
        grad_upb = jnp.sum(grad_hidden.astype(jnp.float32), axis=0).reshape(full_upb.shape)
        grad_two = lax.psum(
            jnp.einsum(
                "tf,df->td", grad_hidden, full_up, preferred_element_type=jnp.float32
            ).astype(jnp.bfloat16),
            "head",
        ).astype(jnp.float32)
        grad_middle = grad_out + norm_back(grad_two, unit_two, inverse_two, gains32[1])
        grad_attended = grad_middle.astype(jnp.bfloat16)
        grad_out_t = jnp.einsum(
            "td,tf->df", grad_attended, mixed_out, preferred_element_type=jnp.float32
        )
        grad_mixed = jnp.einsum(
            "td,df->tf", grad_attended, full_out, preferred_element_type=jnp.float32
        ).reshape(local_rows, heads_here, DH)
        grad_numer32, grad_denom = finish_back(grad_mixed)
        grad_numer = grad_numer32.astype(jnp.bfloat16)
        grad_numer_wide = grad_numer.astype(jnp.float32)
        grad_scores = (
            (
                jnp.einsum(
                    "the,jhe->htj", grad_numer, value_feat, preferred_element_type=jnp.float32
                )
                + grad_denom.T[:, :, None]
            )
            * same_item[None]
        ).astype(jnp.bfloat16)
        carried_query = query32 * carried[:, None, None]
        grad_query = jnp.einsum(
            "htj,jhd->thd", grad_scores, key_feat, preferred_element_type=jnp.float32
        ) + carried[:, None, None] * (
            jnp.einsum("hde,the->thd", state_in, grad_numer_wide, precision=highest)
            + grad_denom[:, :, None] * total_in[None]
        )
        grad_key = jnp.einsum(
            "htj,thd->jhd", grad_scores, query_feat, preferred_element_type=jnp.float32
        )
        grad_value = jnp.einsum(
            "htj,the->jhe", scores_low, grad_numer, preferred_element_type=jnp.float32
        )
        grad_state_in = jnp.einsum(
            "thd,the->hde", carried_query, grad_numer_wide, precision=highest
        )
        grad_total_in = jnp.einsum("thd,th->hd", carried_query, grad_denom, precision=highest)
        grad_state_loc, grad_total_loc, passed_back = entering_2(
            (grad_state_in, grad_total_in, through), "seq", compose, identity
        )
        tail_three = tail_mask[:, None, None]
        value_wide = value_feat.astype(jnp.float32)
        key_wide = key_feat.astype(jnp.float32)
        grad_key = grad_key + tail_three * (
            jnp.einsum("hde,jhe->jhd", grad_state_loc, value_wide, precision=highest)
            + grad_total_loc[None]
        )
        grad_value = grad_value + tail_three * jnp.einsum(
            "jhd,hde->jhe", key_wide, grad_state_loc, precision=highest
        )
        ignored, feature_back = jax.vjp(features, projected[:, :2])
        grad_features = jnp.stack(
            [
                grad_query.reshape(local_rows, local_width),
                grad_key.reshape(local_rows, local_width) * keep32[:, None],
            ],
            axis=1,
        )
        grad_pair = feature_back(grad_features)[0]
        grad_projected = jnp.concatenate(
            [grad_pair, grad_value.reshape(local_rows, 1, local_width)], axis=1
        ).astype(jnp.bfloat16)
        grad_qkv = jnp.einsum(
            "td,tsf->dsf", normed, grad_projected, preferred_element_type=jnp.float32
        )
        grad_one = lax.psum(
            jnp.einsum(
                "tsf,dsf->td", grad_projected, full_qkv, preferred_element_type=jnp.float32
            ).astype(jnp.bfloat16),
            "head",
        ).astype(jnp.float32)
        grad_inputs = grad_middle + norm_back(grad_one, unit_one, inverse_one, gains32[0])
        input_grads.append(own_columns(grad_inputs))
        grad_gains = jnp.stack(
            [jnp.sum(grad_one * unit_one, axis=0), jnp.sum(grad_two * unit_two, axis=0)]
        )
        grad_biases = jnp.stack(
            [jnp.sum(grad_one, axis=0), jnp.sum(grad_two, axis=0), jnp.sum(grad_out, axis=0)]
        )
        pieces = (
            lax.psum_scatter(grad_qkv, "seq", scatter_dimension=0, tiled=True),
            lax.psum_scatter(grad_out_t, "seq", scatter_dimension=0, tiled=True),
            lax.psum_scatter(grad_up, "seq", scatter_dimension=0, tiled=True),
            lax.psum_scatter(grad_down, "seq", scatter_dimension=0, tiled=True),
            lax.psum_scatter(grad_gains, "seq", scatter_dimension=1, tiled=True),
            lax.psum_scatter(grad_biases, "seq", scatter_dimension=1, tiled=True),
            lax.psum_scatter(grad_upb, "seq", scatter_dimension=1, tiled=True),
        )
        shard_sums = pieces if shard_sums is None else jax.tree.map(jnp.add, shard_sums, pieces)
    return (
        jnp.stack(results),
        jnp.stack(input_grads),
        shard_sums[0],
        shard_sums[1],
        shard_sums[2],
        shard_sums[3],
        shard_sums[4],
        shard_sums[5],
        shard_sums[6],
    )


def solution(mesh):
    in_specs = (
        P(None, "seq", "head"),
        P(None, "seq", "head"),
        P("seq", None, "head"),
        P("seq", "head"),
        P("seq", "head"),
        P("seq", "head"),
        P(None, "seq"),
        P(None, "seq"),
        P("head", "seq"),
        P(),
        P(None, "seq"),
    )
    out_specs = (
        P(None, "seq", "head"),
        P(None, "seq", "head"),
        P("seq", None, "head"),
        P("seq", "head"),
        P("seq", "head"),
        P("seq", "head"),
        P(None, "seq"),
        P(None, "seq"),
        P("head", "seq"),
    )
    return jax.shard_map(
        on_device, mesh=mesh, in_specs=in_specs, out_specs=out_specs, check_vma=False
    )
```

profile of v0, /device:TPU:0, one launch (start us, length us, event | category | flops | bytes accessed | tf_op | source)
XLA Modules:
  0.0 1235.3 jit_solution(5156586911502949135)
XLA Ops:
  12.3 22.6 %all_gather.102 = bf16[3,1024]{1,0:T(4,128)(2,1)S(1)} all-gather(bf16[3,128]{1,0:T(4,128)(2,1)} %param.26), channel_id=1, replica_groups=mesh['seq'=8,'head'=4] {'seq'}, dimensions={1}, use_global_device_ids=true | all-gather | bytes 6912 | tf_op jit(solution)/shard_map/all_gather | solution.py:120
  68.1 19.6 %all-reduce.2 = (bf16[8]{0:T(256)(128)(2,1)S(1)}, bf16[8]{0:T(256)(128)(2,1)}) all-reduce(bf16[8]{0:T(256)(128)(2,1)S(1)} %dynamic-update-slice.1, bf16[8]{0:T(256)(128)(2,1)S(1)} %dynamic-update-slice), channel_id=1, replica_groups=mesh['seq'=8,'head'=4] {'seq'}, use_global_device_ids=true, to_apply=%add.1 | all-reduce | flops 16 | bytes 64
  96.1 31.3 %all_gather.109 = bf16[1024,256]{1,0:T(8,128)(2,1)S(1)} all-gather(bf16[128,256]{1,0:T(8,128)(2,1)S(1)} %copy-done.65), channel_id=1, replica_groups=mesh['seq'=8,'head'=4] {'seq'}, dimensions={0}, use_global_device_ids=true | all-gather | bytes 589824 | tf_op jit(solution)/shard_map/all_gather | solution.py:116
  131.2 31.3 %all-gather.3 = bf16[32,64,64]{2,1,0:T(8,128)(2,1)S(1)} all-gather(bf16[4,64,64]{2,1,0:T(8,128)(2,1)S(1)} %convolution_convert_fusion.8), channel_id=5, replica_groups=mesh['seq'=8,'head'=4] {'seq'}, dimensions={0}, use_global_device_ids=true | all-gather | bytes 294912 | tf_op jit(solution)/shard_map/all_gather | solution.py:16
  184.4 37.8 %all-gather.1 = bf16[32,64,64]{2,1,0:T(8,128)(2,1)S(1)} all-gather(bf16[4,64,64]{2,1,0:T(8,128)(2,1)S(1)} %convolution_convert_fusion.9), channel_id=3, replica_groups=mesh['seq'=8,'head'=4] {'seq'}, dimensions={0}, use_global_device_ids=true | all-gather | bytes 294912 | tf_op jit(solution)/shard_map/all_gather | solution.py:16
  222.3 21.8 %all_gather.108 = bf16[8,4,64]{2,1,0:T(4,128)(2,1)} all-gather(bf16[1,4,64]{2,1,0:T(4,128)(2,1)S(1)} %all_gather.107), channel_id=1, replica_groups=mesh['seq'=8,'head'=4] {'seq'}, dimensions={0}, use_global_device_ids=true | all-gather | bytes 4608 | tf_op jit(solution)/shard_map/all_gather | solution.py:16
  253.1 33.8 %all_gather.111 = bf16[1,1024]{1,0:T(2,128)(2,1)S(1)} all-gather(bf16[1,128]{1,0:T(2,128)(2,1)S(1)} %copy-done.127), channel_id=1, replica_groups=mesh['seq'=8,'head'=4] {'seq'}, dimensions={1}, use_global_device_ids=true | all-gather | bytes 2304 | tf_op jit(solution)/shard_map/all_gather | solution.py:121
  311.7 45.1 %all-gather.18.cloned.1.call-done = bf16[1024,1024]{1,0:T(8,128)(2,1)} async-done(((bf16[128,1024]{1,0:T(8,128)(2,1)}), bf16[1024,1024]{1,0:T(8,128)(2,1)}) %all-gather.18.cloned.1.call-update) | async-done | bytes 2097168 | tf_op jit(solution)/shard_map/all_gather | solution.py:117
  362.1 44.6 %all-gather.20.cloned.1.call-done = bf16[1024,1024]{1,0:T(8,128)(2,1)} async-done(((bf16[128,1024]{1,0:T(8,128)(2,1)}), bf16[1024,1024]{1,0:T(8,128)(2,1)}) %all-gather.20.cloned.1.call-update) | async-done | bytes 2097168 | tf_op jit(solution)/shard_map/all_gather | solution.py:118
  417.0 33.4 %all-reduce.12.cloned.1.call-done = (bf16[256,1024]{1,0:T(8,128)(2,1)}, bf16[256,1024]{1,0:T(8,128)(2,1)}) async-done(((bf16[256,1024]{1,0:T(8,128)(2,1)}, bf16[256,1024]{1,0:T(8,128)(2,1)}), (bf16[256,1024]{1,0:T(8,128)(2,1)}, bf16[256,1024]{1,0:T(8,128)(2,1)})) %all-reduce.12.cloned.1.call-update) | async-done | bytes 1048592 | tf_op jit(solution)/shard_map/psum | solution.py:207
  464.5 31.7 %all-gather.8 = bf16[32,64,64]{2,1,0:T(8,128)(2,1)S(1)} all-gather(bf16[4,64,64]{2,1,0:T(8,128)(2,1)S(1)} %convolution_convert_fusion.6), channel_id=10, replica_groups=mesh['seq'=8,'head'=4] {'seq'}, dimensions={0}, use_global_device_ids=true | all-gather | bytes 294912 | tf_op jit(solution)/shard_map/all_gather | solution.py:38
  498.1 20.4 %all-gather.11 = bf16[8,4,64]{2,1,0:T(4,128)(2,1)S(1)} all-gather(bf16[1,4,64]{2,1,0:T(4,128)(2,1)S(1)} %convert_bitcast_fusion.2), channel_id=11, replica_groups=mesh['seq'=8,'head'=4] {'seq'}, dimensions={0}, use_global_device_ids=true | all-gather | bytes 4608 | tf_op jit(solution)/shard_map/all_gather | solution.py:38
  518.5 25.5 %while.67 = (s32[]{:T(128)}, f32[4,64,64]{2,1,0:T(8,128)S(1)}, f32[4,64]{1,0:T(4,128)}, s32[]{:T(128)}, bf16[8,4,64,64]{3,2,1,0:T(8,128)(2,1)S(1)}, /*index=5*/b...) while((s32[]{:T(128)}, f32[4,64,64]{2,1,0:T(8,128)S(1)}, ...), condition=%wide.region_38.39_spmd.clone, body=%wide.region_37.38_spmd.clone.sunk | while | flops 83209 | bytes 166615 | solution.py:56
  547.4 31.5 %all-gather.5 = bf16[32,64,64]{2,1,0:T(8,128)(2,1)S(1)} all-gather(bf16[4,64,64]{2,1,0:T(8,128)(2,1)S(1)} %copy-done.58), channel_id=7, replica_groups=mesh['seq'=8,'head'=4] {'seq'}, dimensions={0}, use_global_device_ids=true | all-gather | bytes 294912 | tf_op jit(solution)/shard_map/all_gather | solution.py:38
  634.0 22.5 %all-reduce.10.cloned.1.call-done = (bf16[256,1024]{1,0:T(8,128)(2,1)}, bf16[256,1024]{1,0:T(8,128)(2,1)}) async-done(((bf16[256,1024]{1,0:T(8,128)(2,1)}, bf16[256,1024]{1,0:T(8,128)(2,1)}), (bf16[256,1024]{1,0:T(8,128)(2,1)}, bf16[256,1024]{1,0:T(8,128)(2,1)})) %all-reduce.10.cloned.1.call-update) | async-done | bytes 1048592 | tf_op jit(solution)/shard_map/psum | solution.py:278
  683.6 38.9 %reduce-scatter.32.cloned.1.call-done = f32[128,1]{1,0:T(8,128)} async-done(((f32[1024,1]{1,0:T(8,128)}), f32[128,1]{1,0:T(8,128)}) %reduce-scatter.32.cloned.1.call-update) | async-done | bytes 528
  727.3 18.9 %reduce-scatter.16.cloned.1.call-done = bf16[256,256]{1,0:T(8,128)(2,1)} async-done(((bf16[256,1024]{1,0:T(8,128)(2,1)}), bf16[256,256]{1,0:T(8,128)(2,1)}) %reduce-scatter.16.cloned.1.call-update) | async-done | bytes 131088 | tf_op jit(solution)/shard_map/reduce_scatter | solution.py:186
  746.3 24.9 %reduce-scatter.18.cloned.1.call-done = bf16[256,256]{1,0:T(8,128)(2,1)} async-done(((bf16[256,1024]{1,0:T(8,128)(2,1)}), bf16[256,256]{1,0:T(8,128)(2,1)}) %reduce-scatter.18.cloned.1.call-update) | async-done | bytes 131088 | tf_op jit(solution)/shard_map/reduce_scatter | solution.py:186
  773.2 63.1 %reduce-scatter.28.cloned.1.call-done = f32[128,2]{1,0:T(8,128)} async-done(((f32[1024,2]{1,0:T(8,128)}), f32[128,2]{1,0:T(8,128)}) %reduce-scatter.28.cloned.1.call-update) | async-done | bytes 1040
  837.8 63.2 %reduce-scatter.30.cloned.1.call-done = f32[128,3]{1,0:T(8,128)} async-done(((f32[1024,3]{1,0:T(8,128)}), f32[128,3]{1,0:T(8,128)}) %reduce-scatter.30.cloned.1.call-update) | async-done | bytes 1552
  902.5 89.5 %reduce-scatter.26.cloned.1.call-done = f32[128,1024]{0,1:T(8,128)} async-done(((f32[1024,1024]{0,1:T(8,128)}), f32[128,1024]{0,1:T(8,128)}) %reduce-scatter.26.cloned.1.call-update) | async-done | bytes 524304 | tf_op jit(solution)/shard_map/reduce_scatter | solution.py:296
  994.0 65.6 %reduce-scatter.22.cloned.1.call-done = f32[128,256]{1,0:T(8,128)} async-done(((f32[1024,256]{1,0:T(8,128)}), f32[128,256]{1,0:T(8,128)}) %reduce-scatter.22.cloned.1.call-update) | async-done | bytes 131088 | tf_op jit(solution)/shard_map/reduce_scatter | solution.py:294
  1059.6 78.1 %reduce-scatter.20.cloned.1.call-done = f32[128,3,256]{2,0,1:T(8,128)} async-done(((f32[1024,3,256]{2,0,1:T(8,128)}), f32[128,3,256]{2,0,1:T(8,128)}) %reduce-scatter.20.cloned.1.call-update) | async-done | bytes 393232 | tf_op jit(solution)/shard_map/reduce_scatter | solution.py:293
  1137.7 91.1 %reduce-scatter.24.cloned.1.call-done = f32[128,1024]{1,0:T(8,128)} async-done(((f32[1024,1024]{1,0:T(8,128)}), f32[128,1024]{1,0:T(8,128)}) %reduce-scatter.24.cloned.1.call-update) | async-done | bytes 524304 | tf_op jit(solution)/shard_map/reduce_scatter | solution.py:295
  (516 shorter events, 264.6 us)
Async XLA Ops:
  7.2 120.5 %all-gather.16.cloned.1.call-start = ((), (), s32[]{:S(2)}) async-start(), calls=%async_computation.9 | async-start | bytes 1769472 | tf_op jit(solution)/shard_map/all_gather | solution.py:115
  9.0 87.1 %copy-start.65 = (bf16[128,256]{1,0:T(8,128)(2,1)S(1)}, bf16[128,256]{1,0:T(8,128)(2,1)}, u32[]{:S(2)}) copy-start(bf16[128,256]{1,0:T(8,128)(2,1)} %param.22) | copy-start | bytes 196612
  9.0 297.1 %all-reduce.14.cloned.1.call-start = ((), (), s32[]{:S(2)}) async-start(), calls=%async_computation.23 | async-start | bytes 2097152 | tf_op jit(solution)/shard_map/psum | solution.py:174
  61.5 117.9 %copy-start.89 = (f32[256]{0:T(256)}, f32[256]{0:T(256)S(1)}, u32[]{:S(2)}) copy-start(f32[256]{0:T(256)S(1)} %get-tuple-element.663) | copy-start | bytes 3076
  95.2 85.7 %copy-start.107 = (f32[256]{0:T(256)}, f32[256]{0:T(256)S(1)}, u32[]{:S(2)}) copy-start(f32[256]{0:T(256)S(1)} %broadcast_multiply_fusion.11) | copy-start | bytes 3076
  95.5 85.4 %copy-start.98 = (f32[256]{0:T(256)}, f32[256]{0:T(256)S(1)}, u32[]{:S(2)}) copy-start(f32[256]{0:T(256)S(1)} %add_rsqrt_fusion.3) | copy-start | bytes 3076
  95.5 85.4 %copy-start.63 = (f32[1,1024]{1,0:T(1,128)}, f32[1,1024]{1,0:T(1,128)S(1)}, u32[]{:S(2)}) copy-start(f32[1,1024]{1,0:T(1,128)S(1)} %get-tuple-element.702) | copy-start | bytes 12292
  96.1 264.1 %copy-start.73 = (f32[1,1024]{1,0:T(1,128)}, f32[1,1024]{1,0:T(1,128)S(1)}, u32[]{:S(2)}) copy-start(f32[1,1024]{1,0:T(1,128)S(1)} %get-tuple-element.689) | copy-start | bytes 12292
  127.6 116.5 %copy-start.37 = (f32[256,256]{0,1:T(8,128)}, f32[256,256]{0,1:T(8,128)S(1)}, u32[]{:S(2)}) copy-start(f32[256,256]{0,1:T(8,128)S(1)} %fusion.128) | copy-start | bytes 786436
  130.1 116.5 %copy-start.24 = (bf16[256,4,64]{0,2,1:T(8,128)(2,1)}, bf16[256,4,64]{0,2,1:T(8,128)(2,1)S(1)}, u32[]{:S(2)}) copy-start(bf16[256,4,64]{0,2,1:T(8,128)(2,1)S(1)} %fusion.96) | copy-start | bytes 393220
  251.7 105.0 %all-gather.18.cloned.1.call-start = ((), (), s32[]{:S(2)}) async-start(), calls=%async_computation.10 | async-start | bytes 2359296 | tf_op jit(solution)/shard_map/all_gather | solution.py:117
  252.4 154.3 %all-gather.20.cloned.1.call-start = ((), (), s32[]{:S(2)}) async-start(), calls=%async_computation.11 | async-start | bytes 2359296 | tf_op jit(solution)/shard_map/all_gather | solution.py:118
  253.0 197.4 %all-reduce.12.cloned.1.call-start = ((), (), s32[]{:S(2)}) async-start(), calls=%async_computation.22 | async-start | bytes 2097152 | tf_op jit(solution)/shard_map/psum | solution.py:207
  295.8 110.9 %copy-start.6 = (bf16[1,256,1024]{2,1,0:T(8,128)(2,1)}, bf16[1,256,1024]{2,1,0:T(8,128)(2,1)S(1)}, u32[]{:S(2)}) copy-start(bf16[1,256,1024]{2,1,0:T(8,128)(2,1)S(1)} %all-gather.7) | copy-start | bytes 1572868
  415.6 240.8 %all-reduce.10.cloned.1.call-start = ((), (), s32[]{:S(2)}) async-start(), calls=%async_computation.21 | async-start | bytes 2097152 | tf_op jit(solution)/shard_map/psum | solution.py:278
  621.6 100.9 %reduce-scatter.32.cloned.1.call-start = ((), (), s32[]{:S(2)}) async-start(), calls=%async_computation.20 | async-start | bytes 589824
  622.8 123.5 %reduce-scatter.16.cloned.1.call-start = ((), (), s32[]{:S(2)}) async-start(), calls=%async_computation.12 | async-start | bytes 655360 | tf_op jit(solution)/shard_map/reduce_scatter | solution.py:186
  626.1 145.1 %reduce-scatter.18.cloned.1.call-start = ((), (), s32[]{:S(2)}) async-start(), calls=%async_computation.13 | async-start | bytes 655360 | tf_op jit(solution)/shard_map/reduce_scatter | solution.py:186
  629.8 206.5 %reduce-scatter.28.cloned.1.call-start = ((), (), s32[]{:S(2)}) async-start(), calls=%async_computation.18 | async-start | bytes 589824
  662.3 238.7 %reduce-scatter.30.cloned.1.call-start = ((), (), s32[]{:S(2)}) async-start(), calls=%async_computation.19 | async-start | bytes 589824
  663.5 328.5 %reduce-scatter.26.cloned.1.call-start = ((), (), s32[]{:S(2)}) async-start(), calls=%async_computation.17 | async-start | bytes 4718592 | tf_op jit(solution)/shard_map/reduce_scatter | solution.py:296
  669.1 390.5 %reduce-scatter.22.cloned.1.call-start = ((), (), s32[]{:S(2)}) async-start(), calls=%async_computation.15 | async-start | bytes 1179648 | tf_op jit(solution)/shard_map/reduce_scatter | solution.py:294
  672.9 464.8 %reduce-scatter.20.cloned.1.call-start = ((), (), s32[]{:S(2)}) async-start(), calls=%async_computation.14 | async-start | bytes 3538944 | tf_op jit(solution)/shard_map/reduce_scatter | solution.py:293
  677.3 551.5 %reduce-scatter.24.cloned.1.call-start = ((), (), s32[]{:S(2)}) async-start(), calls=%async_computation.16 | async-start | bytes 4718592 | tf_op jit(solution)/shard_map/reduce_scatter | solution.py:295
  (124 other events, 1820.1 us)
Sparse Core Ops, SparseCore 0:
  10.7 48.0 all-gather.15
  251.8 53.1 all-reduce.13
  307.3 49.3 all-gather.17
  358.9 47.7 all-gather.19
  415.7 34.6 all-reduce.11
  621.7 34.6 all-reduce.9
  660.1 62.3 reduce-scatter.31
  725.6 20.6 reduce-scatter.15
  749.5 21.6 reduce-scatter.17
  774.4 61.8 reduce-scatter.27
  840.0 60.9 reduce-scatter.29
  904.4 87.4 reduce-scatter.25
  996.3 63.2 reduce-scatter.21
  1063.6 74.0 reduce-scatter.19
  1141.8 87.0 reduce-scatter.23
where the time goes:
time: 1240 us
  waiting for transfers between devices  680 us (55%)
  blocking collectives  363 us (29%)
  matrix products  71.1 us (6%)
  other arithmetic  47.1 us (4%)
  local copies, waits for them, and re-layouts  46.7 us (4%)
  between operations  15.7 us (1%)
    unnamed x18, waiting for transfers between devices  167 us
    all_gather x4, blocking collectives, entering(): lax.all_gather(a.astype(kind), axis)  107 us
    all_gather x4, blocking collectives, entering_2(): lax.all_gather(part.astype(kind), axis)  99.9 us
    reduce_scatter x1, waiting for transfers between devices, on_device(): lax.psum_scatter(grad_up, 'seq', scatter_dimension=0, tiled=True)  91.1 us
    reduce_scatter x1, waiting for transfers between devices, on_device(): lax.psum_scatter(grad_down, 'seq', scatter_dimension=0, tiled=True)  89.5 us
    reduce_scatter x1, waiting for transfers between devices, on_device(): lax.psum_scatter(grad_qkv, 'seq', scatter_dimension=0, tiled=True)  78.1 us
    reduce_scatter x1, waiting for transfers between devices, on_device(): lax.psum_scatter(grad_out_t, 'seq', scatter_dimension=0, tiled=True)  65.6 us
    all_gather x1, waiting for transfers between devices, on_device(): lax.all_gather(w_up, 'seq', axis=0, tiled=True)  45.1 us
  transfers between devices with their start and end apart: 15, of which 13 were waited for; matrix products, arithmetic and copies ran while one was open for 6% of the time, Pallas kernels for 0%

commit v1 on v0

--- a/solution.py
+++ b/solution.py
@@ -1,6 +1,10 @@
+import functools
+
 import jax
 import jax.numpy as jnp
 from jax import lax
+from jax.experimental import pallas as pl
+from jax.experimental.pallas import tpu as pltpu
 from jax.sharding import PartitionSpec as P
 
 DH = 64
@@ -312,6 +316,965 @@
     )
 
 
+MESH = pl.DeviceIdType.MESH
+BF = jnp.bfloat16
+F32 = jnp.float32
+QKV, OUT, UP, DOWN = range(4)
+
+
+def dot_nn(a, b):
+    return lax.dot_general(a, b, (((1,), (0,)), ((), ())), preferred_element_type=F32)
+
+
+def dot_nt(a, b):
+    return lax.dot_general(a, b, (((1,), (1,)), ((), ())), preferred_element_type=F32)
+
+
+def dot_tn(a, b):
+    return lax.dot_general(a, b, (((0,), (0,)), ((), ())), preferred_element_type=F32)
+
+
+def ds(start, size):
+    return pl.ds(pl.multiple_of(start, size), size)
+
+
+def loop(count, body):
+    def step(i, carry):
+        body(i)
+        return carry
+
+    lax.fori_loop(0, count, step, 0)
+
+
+def layout(n, m, batches, rows, width, local, hidden):
+    tokens = batches * rows
+    block = width // n
+    own = tokens // m
+    hops = n // 2
+    heads = local // DH
+    vm = {
+        "xg": ((batches, rows, width), BF),
+        "cg": ((batches, rows, width), BF),
+        "wq": ((3, width, local), BF),
+        "wo": ((width, local), BF),
+        "wu": ((width, hidden), BF),
+        "wd": ((width, hidden), BF),
+        "small": ((8, block), F32),
+        "smallg": ((8, width), F32),
+        "normed": ((tokens, width), BF),
+        "phi_d": ((2, tokens, local), F32),
+        "qf": ((tokens, local), BF),
+        "kf": ((tokens, local), BF),
+        "vf": ((tokens, local), BF),
+        "mask": ((batches, rows, rows), F32),
+        "car": ((batches, rows, local), F32),
+        "tail": ((batches, rows, local), F32),
+        "pmc": ((batches, rows, local), F32),
+        "low": ((batches, rows, heads * rows), BF),
+        "numer": ((tokens, local), F32),
+        "denom": ((tokens, local), F32),
+        "mixed": ((tokens, local), BF),
+        "st_send": ((batches, DH + 16, local), BF),
+        "st_recv": ((2, batches, DH + 16, local), BF),
+        "gs_send": ((batches, DH + 16, local), BF),
+        "gs_recv": ((2, batches, DH + 16, local), BF),
+        "middle": ((own, width), F32),
+        "ntwo": ((tokens, width), BF),
+        "gelu_d": ((tokens, hidden), F32),
+        "activ": ((tokens, hidden), BF),
+        "g_hid": ((tokens, hidden), BF),
+        "branch": ((own, width), F32),
+        "total": ((own, width), F32),
+        "g_mid": ((own, width), F32),
+        "gatt": ((tokens, width), BF),
+        "g_attn": ((tokens, local), F32),
+        "g_num": ((tokens, local), BF),
+        "g_den": ((tokens, local), F32),
+        "gq": ((tokens, local), F32),
+        "gk": ((tokens, local), F32),
+        "gv": ((tokens, local), F32),
+        "gproj": ((3, tokens, local), BF),
+        "h_s1": ((4, 2, own, width), BF),
+        "h_r1": ((4, 2, own, width), BF),
+        "h_acc": ((4, 2, own, width), F32),
+        "h_s2": ((4, own, width), BF),
+        "h_r2": ((4, own, width), BF),
+        "rq_s": ((2, 2, hops, 3, block, local // 2), BF),
+        "rq_r": ((2, 2, hops, 3, block, local // 2), BF),
+        "ro_s": ((2, 2, hops, block, local // 2), BF),
+        "ro_r": ((2, 2, hops, block, local // 2), BF),
+        "ru_s": ((2, 2, hops, block, hidden // 2), BF),
+        "ru_r": ((2, 2, hops, block, hidden // 2), BF),
+        "rd_s": ((2, 2, hops, block, hidden // 2), BF),
+        "rd_r": ((2, 2, hops, block, hidden // 2), BF),
+        "fq": ((3, block, local), F32),
+        "fo": ((block, local), F32),
+        "fu": ((block, hidden), F32),
+        "fd": ((block, hidden), F32),
+        "hs_recv": ((m, 8, width), F32),
+        "hs_send": ((8, width), F32),
+        "upb": ((1, hidden), F32),
+        "sg": ((8, width), F32),
+        "ss_recv": ((n, 8, block), F32),
+        "a_rows": ((own, width), F32),
+        "i_rows": ((own, width), F32),
+    }
+    sems = {
+        "ag_s": (4, 2, 2, hops),
+        "ag_r": (4, 2, 2, hops),
+        "rs_s": (4, 2, 2, hops),
+        "rs_r": (4, 2, 2, hops),
+        "hg_s": (4, 3),
+        "hg_r": (4, 3),
+        "hr_s": (4, 2),
+        "hr_r": (4, 2),
+        "st_s": (2, 2),
+        "st_r": (2, 2),
+        "sm_s": (n,),
+        "sm_r": (n,),
+        "aa_s": (2, m),
+        "aa_r": (2, m),
+        "hs_s": (m,),
+        "hs_r": (m,),
+        "ss_s": (n,),
+        "ss_r": (n,),
+        "lc": (12,),
+    }
+    return vm, sems
+
+
+class Refs:
+    pass
+
+
+def body(n, m, names, *refs):
+    r = Refs()
+    for name, ref in zip(names, refs):
+        setattr(r, name, ref)
+    batches, rows, width = r.xg.shape
+    tokens = batches * rows
+    own = tokens // m
+    block = width // n
+    local = r.wo.shape[1]
+    hidden = r.wu.shape[1]
+    heads = local // DH
+    hops = n // 2
+    s = lax.axis_index("seq")
+    h = lax.axis_index("head")
+    odd = lax.rem(s, 2)
+    p = (1 - odd) * lax.div(s, 2) + odd * (n - 1 - lax.div(s, 2))
+    lo, hi = lax.rem(h, 2), lax.div(h, 2)
+    pair = h + 1 - 2 * lo
+    cross = lax.rem(h + 2, m)
+
+    def at(place):
+        place = lax.rem(place + 2 * n, n)
+        far = lax.div(place, hops)
+        return (1 - far) * 2 * place + far * (2 * (n - 1 - place) + 1)
+
+    ring = (at(p + 1), at(p - 1))
+    sign = (1, -1)
+
+    def remote(src, dst, send, recv, seq, head):
+        return pltpu.make_async_remote_copy(
+            src_ref=src,
+            dst_ref=dst,
+            send_sem=send,
+            recv_sem=recv,
+            device_id=(seq, head),
+            device_id_type=MESH,
+        )
+
+    sent = []
+
+    def launch(copy):
+        copy.start()
+        sent.append(copy)
+
+    r.small[...] = jnp.zeros_like(r.small)
+    r.small[0:2, :] = r.gains[...].astype(F32)
+    r.small[2:5, :] = r.biases[...].astype(F32)
+    r.small[5:6, :] = r.up_bias[...].astype(F32)
+
+    barrier = pltpu.get_barrier_semaphore()
+    for i in range(1, n):
+        pl.semaphore_signal(
+            barrier, inc=1, device_id=(lax.rem(s + i, n), h), device_id_type=MESH
+        )
+    for i in range(1, m):
+        pl.semaphore_signal(
+            barrier, inc=1, device_id=(s, lax.rem(h + i, m)), device_id_type=MESH
+        )
+    pl.semaphore_wait(barrier, n - 1 + m - 1)
+
+    shards = (r.w_qkv, r.w_out, r.w_up, r.w_down)
+    gathered = (r.wq, r.wo, r.wu, r.wd)
+
+    def shard_piece(w, piece):
+        half = shards[w].shape[-1] // 2
+        cols = pl.ds(piece * half, half)
+        return shards[w].at[:, :, cols] if w == QKV else shards[w].at[:, cols]
+
+    def full_piece(w, owner, piece):
+        half = gathered[w].shape[-1] // 2
+        cols = pl.ds(piece * half, half)
+        if w == QKV:
+            return gathered[w].at[:, ds(owner * block, block), cols]
+        return gathered[w].at[ds(owner * block, block), cols]
+
+    def lanes():
+        return [(piece, d) for piece in (0, 1) for d in (0, 1)]
+
+    def reach(piece, d):
+        return hops if piece == d else hops - 1
+
+    def ag_send(w, j):
+        for piece, d in lanes():
+            if j < reach(piece, d):
+                owner = at(p - sign[d] * j)
+                src = shard_piece(w, piece) if j == 0 else full_piece(w, owner, piece)
+                launch(
+                    remote(
+                        src,
+                        full_piece(w, owner, piece),
+                        r.ag_s.at[w, piece, d, j],
+                        r.ag_r.at[w, piece, d, j],
+                        ring[d],
+                        h,
+                    )
+                )
+
+    def ag_wait(w, j):
+        for piece, d in lanes():
+            if j < reach(piece, d):
+                view = full_piece(w, at(p - sign[d] * (j + 1)), piece)
+                remote(
+                    view, view, r.ag_s.at[w, piece, d, j], r.ag_r.at[w, piece, d, j], ring[d], h
+                ).wait_recv()
+
+    def ag_pass(w, j):
+        ag_wait(w, j)
+        ag_send(w, j + 1)
+
+    def hg_view(k, who):
+        if k < 2:
+            return (r.xg, r.cg)[k].at[:, :, ds(who * local, local)]
+        return (r.ntwo, r.gatt)[k - 2].at[ds(who * own, own), :]
+
+    def hg_copy(k, i, src, who, to):
+        return remote(src, hg_view(k, who), r.hg_s.at[k, i], r.hg_r.at[k, i], s, to)
+
+    def hg_start(k, src):
+        launch(hg_copy(k, 1, src, h, cross))
+        launch(hg_copy(k, 0, src, h, pair))
+
+    def hg_forward(k):
+        view = hg_view(k, cross)
+        hg_copy(k, 1, view, cross, cross).wait_recv()
+        launch(hg_copy(k, 2, view, cross, pair))
+
+    def hg_finish(k):
+        view = hg_view(k, pair)
+        hg_copy(k, 0, view, pair, pair).wait_recv()
+        across = lax.rem(pair + 2, m)
+        view = hg_view(k, across)
+        hg_copy(k, 2, view, across, pair).wait_recv()
+
+    def hr_rows(who):
+        return ds(who * own, own)
+
+    def hr_first(k, term):
+        for q in (0, 1):
+            who = 2 * q + 1 - lo
+            term(hr_rows(who), lambda cols, v, q=q: put(r.h_s1.at[k, q], cols, v))
+        launch(remote(r.h_s1.at[k], r.h_r1.at[k], r.hr_s.at[k, 0], r.hr_r.at[k, 0], s, pair))
+        for q in (0, 1):
+            who = 2 * q + lo
+            term(hr_rows(who), lambda cols, v, q=q: put(r.h_acc.at[k, q], cols, v))
+
+    def put(ref, cols, value):
+        ref[:, cols] = value.astype(ref.dtype)
+
+    def hr_second(k):
+        remote(
+            r.h_s1.at[k], r.h_r1.at[k], r.hr_s.at[k, 0], r.hr_r.at[k, 0], s, pair
+        ).wait_recv()
+        tile = 32
+
+        def away(i):
+            rw = ds(i * tile, tile)
+            r.h_s2[k, rw, :] = (
+                r.h_acc[k, 1 - hi, rw, :] + r.h_r1[k, 1 - hi, rw, :].astype(F32)
+            ).astype(BF)
+
+        loop(own // tile, away)
+        launch(remote(r.h_s2.at[k], r.h_r2.at[k], r.hr_s.at[k, 1], r.hr_r.at[k, 1], s, cross))
+
+    def hr_wait(k):
+        remote(
+            r.h_s2.at[k], r.h_r2.at[k], r.hr_s.at[k, 1], r.hr_r.at[k, 1], s, cross
+        ).wait_recv()
+
+    def hr_value(k, rw):
+        return (
+            r.h_acc[k, hi, rw, :]
+            + r.h_r1[k, hi, rw, :].astype(F32)
+            + r.h_r2[k, rw, :].astype(F32)
+        )
+
+    def rs_term(w, owner, piece):
+        cols = ds(owner * block, block)
+        if w == DOWN:
+            left = r.cg[:, :, cols].reshape(tokens, block)
+            half = hidden // 2
+            return [dot_tn(left, r.activ[:, pl.ds(piece * half, half)])]
+        if w == UP:
+            half = hidden // 2
+            return [dot_tn(r.ntwo[:, cols], r.g_hid[:, pl.ds(piece * half, half)])]
+        half = local // 2
+        if w == OUT:
+            return [dot_tn(r.gatt[:, cols], r.mixed[:, pl.ds(piece * half, half)])]
+        left = r.normed[:, cols]
+        return [dot_tn(left, r.gproj[i, :, pl.ds(piece * half, half)]) for i in range(3)]
+
+    rs_send = (r.rq_s, r.ro_s, r.ru_s, r.rd_s)
+    rs_recv = (r.rq_r, r.ro_r, r.ru_r, r.rd_r)
+
+    def rs_copy(w, piece, d, j):
+        return remote(
+            rs_send[w].at[piece, d, j],
+            rs_recv[w].at[piece, d, j],
+            r.rs_s.at[w, piece, d, j],
+            r.rs_r.at[w, piece, d, j],
+            ring[d],
+            h,
+        )
+
+    def rs_round(w, step):
+        waiting = None
+        for piece, d in lanes():
+            far = reach(piece, d)
+            j = step - (hops - far)
+            if j < 0:
+                continue
+            terms = rs_term(w, at(p + sign[d] * (far - j)), piece)
+            if j > 0:
+                rs_copy(w, piece, d, j - 1).wait_recv()
+            for i, v in enumerate(terms):
+                where = (piece, d, j, i) if w == QKV else (piece, d, j)
+                before = (piece, d, j - 1, i) if w == QKV else (piece, d, j - 1)
+                if j > 0:
+                    v = v + rs_recv[w][before].astype(F32)
+                rs_send[w][where] = v.astype(BF)
+            if waiting is not None:
+                launch(waiting)
+            waiting = rs_copy(w, piece, d, j)
+        launch(waiting)
+
+    finals = (r.fq, r.fo, r.fu, r.fd)
+    results = (r.gq_o, r.go_o, r.gu_o, r.gd_o)
+    local_copies = []
+
+    def rs_final(w):
+        for piece in (0, 1):
+            terms = rs_term(w, s, piece)
+            for d in (0, 1):
+                rs_copy(w, piece, d, reach(piece, d) - 1).wait_recv()
+            half = finals[w].shape[-1] // 2
+            cols = pl.ds(piece * half, half)
+            for i, v in enumerate(terms):
+                for d in (0, 1):
+                    j = reach(piece, d) - 1
+                    where = (piece, d, j, i) if w == QKV else (piece, d, j)
+                    v = v + rs_recv[w][where].astype(F32)
+                if w == QKV:
+                    finals[w][i, :, cols] = v
+                else:
+                    finals[w][:, cols] = v
+        copy = pltpu.make_async_copy(finals[w], results[w], r.lc.at[w])
+        copy.start()
+        local_copies.append(copy)
+
+    def turn(k, src, dst):
+        where = (hi, ds(lo * own, own))
+        for i in range(1, m):
+            to = lax.rem(h + i, m)
+            launch(
+                remote(
+                    src.at[:, ds(to * local, local)],
+                    dst.at[where[0], where[1], :],
+                    r.aa_s.at[k, i],
+                    r.aa_r.at[k, i],
+                    s,
+                    to,
+                )
+            )
+        copy = pltpu.make_async_copy(
+            src.at[:, ds(h * local, local)], dst.at[where[0], where[1], :], r.lc.at[4 + k]
+        )
+        copy.start()
+        local_copies.append(copy)
+
+    def turn_wait(k, src, dst):
+        for i in range(1, m):
+            who = lax.rem(h + m - i, m)
+            remote(
+                src.at[:, ds(h * local, local)],
+                dst.at[lax.div(who, 2), ds(lax.rem(who, 2) * own, own), :],
+                r.aa_s.at[k, i],
+                r.aa_r.at[k, i],
+                s,
+                who,
+            ).wait_recv()
+
+    ag_send(QKV, 0)
+    ag_send(OUT, 0)
+    hg_start(0, r.tok)
+    for i in range(1, n):
+        to = lax.rem(s + i, n)
+        launch(
+            remote(
+                r.small,
+                r.smallg.at[:, ds(s * block, block)],
+                r.sm_s.at[i],
+                r.sm_r.at[i],
+                to,
+                h,
+            )
+        )
+    own_copies = [
+        pltpu.make_async_copy(r.tok, hg_view(0, h), r.lc.at[6]),
+        pltpu.make_async_copy(r.cot, hg_view(1, h), r.lc.at[7]),
+        pltpu.make_async_copy(r.w_qkv, r.wq.at[:, ds(s * block, block), :], r.lc.at[8]),
+        pltpu.make_async_copy(r.w_out, r.wo.at[ds(s * block, block), :], r.lc.at[9]),
+        pltpu.make_async_copy(r.w_up, r.wu.at[ds(s * block, block), :], r.lc.at[10]),
+        pltpu.make_async_copy(r.w_down, r.wd.at[ds(s * block, block), :], r.lc.at[11]),
+    ]
+    for copy in own_copies:
+        copy.start()
+    hg_start(1, r.cot)
+
+    first = s * rows
+    row_at = lax.broadcasted_iota(jnp.int32, (rows, local), 0)
+    lane_at = lax.broadcasted_iota(jnp.int32, (rows, rows), 1)
+    square = lax.broadcasted_iota(jnp.int32, (local, local), 0)
+    square_lane = lax.broadcasted_iota(jnp.int32, (local, local), 1)
+    same_head = (square // DH) == (square_lane // DH)
+    diagonal = square == square_lane
+    ones = jnp.ones((rows, local), BF)
+    lane_head = lax.broadcasted_iota(jnp.int32, (rows, local), 1) // DH
+    before_thr, after_thr = [], []
+
+    def begin(offsets, place):
+        value = 0
+        for off in offsets:
+            value = jnp.where(off <= place, off, value)
+        return value
+
+    def through(offsets, which):
+        return jnp.where(
+            begin(offsets, which * rows + rows - 1) < which * rows, 1.0, 0.0
+        ).astype(F32)
+
+    for b in range(batches):
+        offsets, running = [], 0
+        for i in range(r.lengths.shape[1]):
+            offsets.append(running)
+            running = running + r.lengths[b, i]
+        start = jnp.zeros((rows, local), jnp.int32)
+        for off in offsets:
+            start = jnp.where(off <= row_at + first, off, start)
+        last = begin(offsets, first + rows - 1)
+        r.mask[b] = jnp.where(
+            (lane_at + first >= start) & (lane_at <= row_at), 1.0, 0.0
+        ).astype(F32)
+        r.car[b] = jnp.where(start < first, 1.0, 0.0).astype(F32)
+        r.tail[b] = jnp.where(start == last, 1.0, 0.0).astype(F32)
+        before_thr.append(through(offsets, lax.rem(s + n - 1, n)))
+        after_thr.append(through(offsets, lax.rem(s + 1, n)))
+        keep = r.pixel[b : b + 1, :].astype(F32)
+        r.pmc[b] = dot_nn(jnp.where(diagonal, keep, 0.0).astype(BF), ones)
+
+    ag_pass(QKV, 0)
+    ag_pass(OUT, 0)
+    hg_forward(0)
+
+    for i in range(1, n):
+        who = lax.rem(s + n - i, n)
+        remote(
+            r.small,
+            r.smallg.at[:, ds(who * block, block)],
+            r.sm_s.at[i],
+            r.sm_r.at[i],
+            who,
+            h,
+        ).wait_recv()
+    r.smallg[:, ds(s * block, block)] = r.small[...]
+    for copy in own_copies:
+        copy.wait()
+    hg_finish(0)
+    gain_one, gain_two = r.smallg[0:1, :], r.smallg[1:2, :]
+    shift_one, shift_two, shift_out = r.smallg[2:3, :], r.smallg[3:4, :], r.smallg[4:5, :]
+    up_shift = r.smallg[5:6, :]
+
+    def unit(values):
+        mean = jnp.mean(values, axis=1, keepdims=True)
+        centered = values - mean
+        inverse = lax.rsqrt(jnp.mean(centered * centered, axis=1, keepdims=True) + epsilon)
+        return centered * inverse, inverse
+
+    tile = 32
+
+    def norm_one(i):
+        b = lax.div(i, rows // tile)
+        rw = ds(lax.rem(i, rows // tile) * tile, tile)
+        u, _ = unit(r.xg[b, rw, :].astype(F32))
+        r.normed[ds(i * tile, tile), :] = (u * gain_one + shift_one).astype(BF)
+
+    ag_pass(QKV, 1)
+    ag_pass(OUT, 1)
+    loop(tokens // tile, norm_one)
+    hg_forward(1)
+    ag_pass(QKV, 2)
+    ag_pass(OUT, 2)
+    ag_send(UP, 0)
+    ag_send(DOWN, 0)
+    hg_finish(1)
+    ag_wait(QKV, 3)
+    ag_wait(OUT, 3)
+
+    tm = 128
+
+    def project(i):
+        rw = ds(i * tm, tm)
+        b = lax.div(i, rows // tm)
+        rb = ds(lax.rem(i, rows // tm) * tm, tm)
+        left = r.normed[rw, :]
+        for kind in (0, 1):
+            v = dot_nn(left, r.wq[kind])
+            low = jnp.exp(jnp.minimum(v, 0.0))
+            f = jnp.where(v > 0.0, v + 1.0, low).astype(BF)
+            r.phi_d[kind, rw, :] = low
+            if kind == 0:
+                r.qf[rw, :] = f
+            else:
+                r.kf[rw, :] = (f.astype(F32) * r.pmc[b, rb, :]).astype(BF)
+        r.vf[rw, :] = dot_nn(left, r.wq[2]).astype(BF)
+
+    loop(tokens // tm, project)
+
+    def fold(matrix, total):
+        kept = jnp.where(same_head, matrix, 0.0)
+        acc = kept[0:DH]
+        for i in range(1, heads):
+            acc = acc + kept[i * DH : (i + 1) * DH]
+        top = lax.broadcasted_iota(jnp.int32, (16, local), 0) == 0
+        return acc.astype(BF), jnp.where(top, total, 0.0).astype(BF)
+
+    def unfold(ref):
+        acc = ref[0:DH, :].astype(F32)
+        wide = jnp.concatenate([acc] * heads, axis=0)
+        return jnp.where(same_head, wide, 0.0).astype(BF)
+
+    def state_send(k, ref, dest, step):
+        for i in (0, 1):
+            to = lax.rem(s + n + step * (i + 1), n)
+            launch(remote(ref, dest.at[i], r.st_s.at[k, i], r.st_r.at[k, i], to, h))
+
+    def state_wait(k, ref, dest, step):
+        for i in (0, 1):
+            to = lax.rem(s + n + step * (i + 1), n)
+            remote(ref, dest.at[i], r.st_s.at[k, i], r.st_r.at[k, i], to, h).wait_recv()
+
+    def rows_of(b):
+        return pl.ds(b * rows, rows)
+
+    def by_head(value):
+        return jnp.concatenate(
+            [jnp.where(lane_head == hd, value.astype(F32), 0.0).astype(BF) for hd in range(heads)],
+            axis=0,
+        )
+
+    for b in range(batches):
+        k = r.kf[rows_of(b), :].astype(F32) * r.tail[b]
+        moved = dot_tn(k.astype(BF), r.vf[rows_of(b), :])
+        a, t = fold(moved, jnp.sum(k, axis=0, keepdims=True))
+        r.st_send[b, 0:DH, :] = a
+        r.st_send[b, DH:, :] = t
+    state_send(0, r.st_send, r.st_recv, 1)
+
+    for b in range(batches):
+        q, k = r.qf[rows_of(b), :], r.kf[rows_of(b), :]
+        acc = jnp.zeros((rows, local), F32)
+        for hd in range(heads):
+            sc = dot_nt(jnp.where(lane_head == hd, q.astype(F32), 0.0).astype(BF), k) * r.mask[b]
+            r.low[b, :, hd * rows : (hd + 1) * rows] = sc.astype(BF)
+            acc = acc + jnp.where(lane_head == hd, jnp.sum(sc, axis=1, keepdims=True), 0.0)
+        r.denom[rows_of(b), :] = acc
+        r.numer[rows_of(b), :] = dot_nn(r.low[b], by_head(r.vf[rows_of(b), :]))
+
+    ag_pass(UP, 0)
+    ag_pass(DOWN, 0)
+    state_wait(0, r.st_send, r.st_recv, 1)
+
+    def both(b, value, thr):
+        one = value.astype(F32) * r.car[b]
+        return jnp.concatenate([one.astype(BF), (one * thr).astype(BF)], axis=1)
+
+    for b in range(batches):
+        left = both(b, r.qf[rows_of(b), :], before_thr[b])
+        states = jnp.concatenate([unfold(r.st_recv.at[i, b]) for i in (0, 1)], axis=0)
+        sums = jnp.concatenate(
+            [
+                jnp.where(
+                    same_head,
+                    dot_tn(r.st_recv[i, b, DH:, :], jnp.ones((16, local), BF)),
+                    0.0,
+                ).astype(BF)
+                for i in (0, 1)
+            ],
+            axis=0,
+        )
+        top = r.numer[rows_of(b), :] + dot_nn(left, states)
+        bottom = r.denom[rows_of(b), :] + dot_nn(left, sums)
+        attn = top / jnp.maximum(bottom, 1.0)
+        r.numer[rows_of(b), :] = attn
+        r.denom[rows_of(b), :] = bottom
+        r.mixed[rows_of(b), :] = attn.astype(BF)
+
+    tn = 256
+
+    def product_nt(left_ref, right_ref):
+        def term(rw, store):
+            def part(i):
+                cols = ds(i * tn, tn)
+                store(cols, dot_nt(left_ref[rw, :], right_ref[cols, :]))
+
+            loop(width // tn, part)
+
+        return term
+
+    hr_first(0, product_nt(r.mixed, r.wo))
+    hr_second(0)
+    ag_pass(UP, 1)
+    ag_pass(DOWN, 1)
+    hr_wait(0)
+    mine = h * own
+
+    def x_rows(i):
+        return r.xg[hi, ds(lo * own + i * tile, tile), :].astype(F32)
+
+    def c_rows(i):
+        return r.cg[hi, ds(lo * own + i * tile, tile), :].astype(F32)
+
+    def norm_two(i):
+        rw = ds(i * tile, tile)
+        v = x_rows(i) + hr_value(0, rw)
+        r.middle[rw, :] = v
+        u, _ = unit(v)
+        r.ntwo[ds(mine + i * tile, tile), :] = (u * gain_two + shift_two).astype(BF)
+
+    loop(own // tile, norm_two)
+    hg_start(2, hg_view(2, h))
+    ag_pass(UP, 2)
+    ag_pass(DOWN, 2)
+    hg_forward(2)
+    hg_finish(2)
+    ag_wait(UP, 3)
+
+    ft = 256
+
+    def up(i):
+        rw = ds(lax.div(i, hidden // ft) * tm, tm)
+        cols = ds(lax.rem(i, hidden // ft) * ft, ft)
+        v = dot_nn(r.ntwo[rw, :], r.wu[:, cols]) + r.smallg[5:6, cols]
+        cube = 0.7978845608028654 * (v + 0.044715 * (v * v * v))
+        t = jnp.tanh(cube)
+        r.activ[rw, cols] = (0.5 * v * (1.0 + t)).astype(BF)
+        r.gelu_d[rw, cols] = 0.5 * (1.0 + t) + 0.5 * v * (1.0 - t * t) * (
+            0.7978845608028654 * (1.0 + 3.0 * 0.044715 * (v * v))
+        )
+
+    loop((tokens // tm) * (hidden // ft), up)
+    rs_round(DOWN, 0)
+    ag_wait(DOWN, 3)
+
+    def back(i):
+        rw = ds(lax.div(i, hidden // ft) * tm, tm)
+        cols = ds(lax.rem(i, hidden // ft) * ft, ft)
+        b = lax.div(lax.div(i, hidden // ft), rows // tm)
+        rb = ds(lax.rem(lax.div(i, hidden // ft), rows // tm) * tm, tm)
+        g = dot_nn(r.cg[b, rb, :], r.wd[:, cols])
+        r.g_hid[rw, cols] = (g * r.gelu_d[rw, cols]).astype(BF)
+
+    loop((tokens // tm) * (hidden // ft), back)
+    hr_first(2, product_nt(r.g_hid, r.wu))
+    hr_second(2)
+    rs_round(UP, 0)
+    rs_round(DOWN, 1)
+    hr_wait(2)
+
+    r.hs_send[...] = jnp.zeros_like(r.hs_send)
+
+    def back_norm(g, u, inverse, gain):
+        scaled = g * gain
+        centered = scaled - jnp.mean(scaled, axis=1, keepdims=True)
+        return inverse * (centered - u * jnp.mean(scaled * u, axis=1, keepdims=True))
+
+    def norm_two_back(i):
+        rw = ds(i * tile, tile)
+        g = hr_value(2, rw)
+        u, inverse = unit(r.middle[rw, :])
+        out = c_rows(i)
+        v = out + back_norm(g, u, inverse, gain_two)
+        r.g_mid[rw, :] = v
+        r.gatt[ds(mine + i * tile, tile), :] = v.astype(BF)
+        r.hs_send[1:2, :] += jnp.sum(g * u, axis=0, keepdims=True)
+        r.hs_send[3:4, :] += jnp.sum(g, axis=0, keepdims=True)
+        r.hs_send[4:5, :] += jnp.sum(out, axis=0, keepdims=True)
+
+    loop(own // tile, norm_two_back)
+    hg_start(3, hg_view(3, h))
+    hr_first(1, product_nt(r.activ, r.wd))
+    rs_round(UP, 1)
+    hg_forward(3)
+    hr_second(1)
+    rs_round(DOWN, 2)
+    hg_finish(3)
+
+    def mixed_back(i):
+        rw = ds(i * tm, tm)
+        g = dot_nn(r.gatt[rw, :], r.wo[...])
+        attn, bottom = r.numer[rw, :], r.denom[rw, :]
+        r.g_num[rw, :] = (g / jnp.maximum(bottom, 1.0)).astype(BF)
+        prod = g * attn
+        lh = lane_head[:tm]
+        acc = jnp.zeros((tm, local), F32)
+        for hd in range(heads):
+            acc = acc + jnp.where(
+                lh == hd,
+                jnp.sum(jnp.where(lh == hd, prod, 0.0), axis=1, keepdims=True),
+                0.0,
+            )
+        r.g_den[rw, :] = jnp.where(bottom > 1.0, -acc / jnp.maximum(bottom, 1.0), 0.0)
+
+    loop(tokens // tm, mixed_back)
+
+    for b in range(batches):
+        q = r.qf[rows_of(b), :].astype(F32) * r.car[b]
+        moved = dot_tn(q.astype(BF), r.g_num[rows_of(b), :])
+        a, t = fold(moved, jnp.sum(q * r.g_den[rows_of(b), :], axis=0, keepdims=True))
+        r.gs_send[b, 0:DH, :] = a
+        r.gs_send[b, DH:, :] = t
+    state_send(1, r.gs_send, r.gs_recv, -1)
+    rs_round(OUT, 0)
+
+    def head_lanes(hd, value):
+        return jnp.where(lane_head == hd, value.astype(F32), 0.0).astype(BF)
+
+    for b in range(batches):
+        rw = rows_of(b)
+        gk = jnp.zeros((rows, local), F32)
+        gv = jnp.zeros((rows, local), F32)
+        gq = jnp.zeros((rows, local), F32)
+        for hd in range(heads):
+            gn = head_lanes(hd, r.g_num[rw, :])
+            g = dot_nt(gn, r.vf[rw, :]) + r.g_den[rw, hd * DH : hd * DH + 1]
+            g = (g * r.mask[b]).astype(BF)
+            gq = gq + dot_nn(g, head_lanes(hd, r.kf[rw, :]))
+            gk = gk + dot_tn(g, head_lanes(hd, r.qf[rw, :]))
+            gv = gv + dot_tn(r.low[b, :, hd * rows : (hd + 1) * rows], gn)
+        left = both(b, r.g_num[rw, :], before_thr[b])
+        states = jnp.concatenate([unfold(r.st_recv.at[i, b]) for i in (0, 1)], axis=1)
+        totals = (
+            r.st_recv[0, b, DH : DH + 16, :].astype(F32)[0:1]
+            + before_thr[b] * r.st_recv[1, b, DH : DH + 16, :].astype(F32)[0:1]
+        )
+        gq = gq + dot_nt(left, states) + r.car[b] * r.g_den[rw, :] * totals
+        r.gproj[0, rw, :] = (gq * r.phi_d[0, rw, :]).astype(BF)
+        r.gk[rw, :] = gk
+        r.gv[rw, :] = gv
+
+    rs_round(OUT, 1)
+    rs_round(UP, 2)
+    state_wait(1, r.gs_send, r.gs_recv, -1)
+    for b in range(batches):
+        rw = rows_of(b)
+        thr = after_thr[b]
+        states = [unfold(r.gs_recv.at[i, b]) for i in (0, 1)]
+        totals = (
+            r.gs_recv[0, b, DH : DH + 16, :].astype(F32)[0:1]
+            + thr * r.gs_recv[1, b, DH : DH + 16, :].astype(F32)[0:1]
+        )
+        k = r.kf[rw, :].astype(F32) * r.tail[b]
+        v = r.vf[rw, :].astype(F32) * r.tail[b]
+        k2 = jnp.concatenate([k.astype(BF), (k * thr).astype(BF)], axis=1)
+        v2 = jnp.concatenate([v.astype(BF), (v * thr).astype(BF)], axis=1)
+        gk = r.gk[rw, :] + dot_nt(v2, jnp.concatenate(states, axis=1)) + r.tail[b] * totals
+        gv = r.gv[rw, :] + dot_nn(k2, jnp.concatenate(states, axis=0))
+        r.gproj[1, rw, :] = (gk * r.pmc[b] * r.phi_d[1, rw, :]).astype(BF)
+        r.gproj[2, rw, :] = gv.astype(BF)
+
+    def first_term(rw, store):
+        def part(i):
+            cols = ds(i * tn, tn)
+            v = dot_nt(r.gproj[0, rw, :], r.wq[0, cols, :])
+            for kind in (1, 2):
+                v = v + dot_nt(r.gproj[kind, rw, :], r.wq[kind, cols, :])
+            store(cols, v)
+
+        loop(width // tn, part)
+
+    hr_first(3, first_term)
+    hr_second(3)
+    rs_round(QKV, 0)
+    rs_round(DOWN, 3)
+    rs_round(OUT, 2)
+    rs_round(UP, 3)
+    rs_round(QKV, 1)
+
+    hr_wait(1)
+
+    def finish_rows(i):
+        rw = ds(i * tile, tile)
+        r.a_rows[rw, :] = r.middle[rw, :] + hr_value(1, rw) + shift_out
+
+    loop(own // tile, finish_rows)
+    turn(0, r.a_rows, r.act_o)
+
+    hr_wait(3)
+
+    def norm_one_back(i):
+        rw = ds(i * tile, tile)
+        g = hr_value(3, rw)
+        u, inverse = unit(x_rows(i))
+        r.i_rows[rw, :] = r.g_mid[rw, :] + back_norm(g, u, inverse, gain_one)
+        r.hs_send[0:1, :] += jnp.sum(g * u, axis=0, keepdims=True)
+        r.hs_send[2:3, :] += jnp.sum(g, axis=0, keepdims=True)
+
+    loop(own // tile, norm_one_back)
+    turn(1, r.i_rows, r.ing_o)
+
+    r.hs_recv[h] = r.hs_send[...]
+    for i in range(1, m):
+        launch(
+            remote(r.hs_send, r.hs_recv.at[h], r.hs_s.at[i], r.hs_r.at[i], s, lax.rem(h + i, m))
+        )
+    r.upb[...] = jnp.zeros_like(r.upb)
+
+    def column_sums(i):
+        r.upb[...] += jnp.sum(r.g_hid[ds(i * tile, tile), :].astype(F32), axis=0, keepdims=True)
+
+    loop(tokens // tile, column_sums)
+    rs_round(OUT, 3)
+    rs_round(QKV, 2)
+    for i in range(1, m):
+        who = lax.rem(h + m - i, m)
+        remote(r.hs_send, r.hs_recv.at[who], r.hs_s.at[i], r.hs_r.at[i], s, who).wait_recv()
+    acc = r.hs_recv[0]
+    for i in range(1, m):
+        acc = acc + r.hs_recv[i]
+    r.sg[...] = acc
+    r.sg[5:6, :] = r.upb[...]
+    r.ss_recv[s] = r.sg[:, ds(s * block, block)]
+    rs_final(DOWN)
+    for i in range(1, n):
+        to = lax.rem(s + i, n)
+        launch(
+            remote(
+                r.sg.at[:, ds(to * block, block)],
+                r.ss_recv.at[s],
+                r.ss_s.at[i],
+                r.ss_r.at[i],
+                to,
+                h,
+            )
+        )
+    rs_round(QKV, 3)
+    rs_final(UP)
+    rs_final(OUT)
+    for i in range(1, n):
+        who = lax.rem(s + n - i, n)
+        remote(
+            r.sg.at[:, ds(s * block, block)],
+            r.ss_recv.at[who],
+            r.ss_s.at[i],
+            r.ss_r.at[i],
+            who,
+            h,
+        ).wait_recv()
+    acc = r.ss_recv[0]
+    for i in range(1, n):
+        acc = acc + r.ss_recv[i]
+    r.gg_o[...] = acc[0:2]
+    r.gb_o[...] = acc[2:5]
+    r.gup_o[...] = acc[5:6]
+    rs_final(QKV)
+    turn_wait(0, r.a_rows, r.act_o)
+    turn_wait(1, r.i_rows, r.ing_o)
+    for copy in local_copies:
+        copy.wait()
+    for copy in sent:
+        copy.wait_send()
+
+
+def whole_layer(n, m):
+    def on_each(
+        tokens, cotangent, w_qkv, w_out_t, w_up, w_down_t, gains, biases, up_bias, lengths, pixel_mask
+    ):
+        batches, rows, local = tokens.shape
+        width = w_qkv.shape[0] * n
+        hidden = w_up.shape[1]
+        block = width // n
+        vm, sems = layout(n, m, batches, rows, width, local, hidden)
+        ins = ["tok", "cot", "w_qkv", "w_out", "w_up", "w_down", "gains", "biases", "up_bias", "lengths", "pixel"]
+        outs = ["act_o", "ing_o", "gq_o", "go_o", "gu_o", "gd_o", "gg_o", "gb_o", "gup_o"]
+        anywhere = pl.BlockSpec(memory_space=pl.ANY)
+        in_vmem = pl.BlockSpec(memory_space=pltpu.VMEM)
+        in_smem = pl.BlockSpec(memory_space=pltpu.SMEM)
+
+        def wide(*shape):
+            return jax.ShapeDtypeStruct(shape, F32)
+
+        result = pl.pallas_call(
+            functools.partial(body, n, m, ins + outs + list(vm) + list(sems)),
+            name="layer",
+            out_shape=(
+                wide(batches, rows, local),
+                wide(batches, rows, local),
+                wide(3, block, local),
+                wide(block, local),
+                wide(block, hidden),
+                wide(block, hidden),
+                wide(2, block),
+                wide(3, block),
+                wide(1, block),
+            ),
+            in_specs=[anywhere] * 6 + [in_vmem] * 3 + [in_smem, in_vmem],
+            out_specs=[anywhere] * 6 + [in_vmem] * 3,
+            scratch_shapes=[pltpu.VMEM(shape, kind) for shape, kind in vm.values()]
+            + [pltpu.SemaphoreType.DMA(shape) for shape in sems.values()],
+            compiler_params=pltpu.CompilerParams(
+                collective_id=0, has_side_effects=True, vmem_limit_bytes=66_000_000
+            ),
+        )(
+            tokens,
+            cotangent,
+            jnp.transpose(w_qkv, (1, 0, 2)),
+            w_out_t,
+            w_up,
+            w_down_t,
+            gains,
+            biases,
+            up_bias,
+            lengths,
+            pixel_mask,
+        )
+        return result[:2] + (jnp.transpose(result[2], (1, 0, 2)),) + result[3:]
+
+    return on_each
+
+
 def solution(mesh):
     in_specs = (
         P(None, "seq", "head"),
@@ -337,6 +1300,8 @@
         P(None, "seq"),
         P("head", "seq"),
     )
+    n, m = mesh.shape["seq"], mesh.shape["head"]
+    fits = (n, m) == (8, 4)
     return jax.shard_map(
-        on_device, mesh=mesh, in_specs=in_specs, out_specs=out_specs, check_vma=False
+        whole_layer(n, m) if fits else on_device, mesh=mesh, in_specs=in_specs, out_specs=out_specs, check_vma=False
     )

time: 1240 us -> 168 us (0.14)
  waiting for transfers between devices: 680 us -> 0 us
  blocking collectives: 363 us -> 0 us
  Pallas kernels: 0 us -> 158 us
  matrix products: 71.1 us -> 0 us
  other arithmetic: 47.1 us -> 0 us
  local copies, waits for them, and re-layouts: 46.7 us -> 8.59 us
  between operations: 15.7 us -> 0.67 us
    reduce_scatter x6 -> x0, waiting for transfers between devices: 368 us -> none  [the longest x1 91.1 us: on_device(): lax.psum_scatter(grad_up, 'seq', scatter_dimension=0, tiled=True)]
    all_gather x16 -> x0, blocking collectives: 343 us -> none  [the longest x4 107 us: entering(): lax.all_gather(a.astype(kind), axis)]
    unnamed x18 -> x0, waiting for transfers between devices: 167 us -> none
    pallas_call x0 -> x1, Pallas kernels: none -> 158 us  [on_each(): pl.pallas_call(functools.partial(body, n, m, ins + outs + list(vm) + list...]
    all_gather x3 -> x0, waiting for transfers between devices: 89.7 us -> none  [the longest x1 45.1 us: on_device(): lax.all_gather(w_up, 'seq', axis=0, tiled=True)]
    dot_general x52 -> x0, matrix products: 71.1 us -> none  [the longest x2 9.62 us: on_device(): jnp.einsum('td,tf->df', grad_rows16, activated, preferred_element_type=jn...]
    psum x3 -> x0, waiting for transfers between devices: 55.8 us -> none  [the longest x1 33.4 us: on_device(): lax.psum(jnp.einsum('tf,df->td', grad_hidden, full_up, preferred_element_...]
    dynamic_slice x17 -> x0, local copies, waits for them, and re-layouts: 21.2 us -> none  [the longest x16 20.5 us: hop(): part[at].astype(own.dtype)]
  transfers between devices with their start and end apart: 15 -> 0, of which waited for: 13 -> 0; matrix products, arithmetic and copies ran while one was open for 6% -> 0% of each run, Pallas kernels for 0% -> 0%
where the time goes in v1:
time: 168 us
  Pallas kernels  158 us (94%)
  local copies, waits for them, and re-layouts  8.59 us (5%)
    pallas_call x1, Pallas kernels, on_each(): pl.pallas_call(functools.partial(body, n, m, ins + outs + list(vm) + list...  158 us
    unnamed x25, local copies, waits for them, and re-layouts  8.59 us

profile of v1, /device:TPU:0, one launch (start us, length us, event | category | flops | bytes accessed | tf_op | source)
XLA Modules:
  0.0 167.7 jit_solution(15744451244604419052)
XLA Ops:
  0.6 158.5 %layer.1 = (f32[2,256,256]{2,1,0:T(8,128)}, f32[2,256,256]{2,1,0:T(8,128)}, f32[3,128,256]{2,1,0:T(8,128)}, f32[128,256]{1,0:T(8,128)}, f32[128,1024]{1,0:T(8,12...) custom-call(bf16[2,256,256]{2,1,0:T(8,128)(2,1)} %refs_0_.1, ...), custom_call_target="tpu_custom_call" | custom-call | tf_op jit(solution)/shard_map/layer/pallas_call | solution.py:1239
  159.1 0.0 copy-start.2
  159.1 1.9 %copy.29 = f32[2,256,256]{2,1,0:T(8,128)} copy(f32[2,256,256]{2,1,0:T(8,128)} %get-tuple-element.36) | data formatting | bytes 1048576
  161.1 0.0 copy-done.2
  161.1 0.0 copy-start.3
  161.1 0.8 copy.30
  161.9 0.4 copy-done.3
  162.3 0.0 copy-start.4
  162.3 0.0 copy-start.1
  162.3 0.7 copy.31
  163.0 0.2 copy-done.4
  163.3 0.7 copy.32
  163.9 0.0 copy-done.1
  163.9 0.0 copy-start
  163.9 0.8 copy.33
  164.7 0.4 copy-done
  165.1 0.0 copy-start.6
  165.1 0.8 copy.34
  165.9 0.0 copy-done.6
  165.9 0.6 copy.35
  166.5 0.1 copy-done.5
  166.6 0.6 copy.36
  167.2 0.0 copy-done.7
  167.2 0.5 copy.37
  (2 shorter events, 0.0 us)
Async XLA Ops:
  159.1 1.9 %copy-start.2 = (f32[2,256,256]{2,1,0:T(8,128)S(1)}, f32[2,256,256]{2,1,0:T(8,128)}, u32[]{:S(2)}) copy-start(f32[2,256,256]{2,1,0:T(8,128)} %get-tuple-element.37) | copy-start | bytes 1572868
  161.1 1.2 copy-start.3
  162.3 1.0 copy-start.4
  162.3 1.7 copy-start.1
  163.9 1.2 copy-start
  165.1 0.8 copy-start.6
  165.9 0.7 copy-start.5
  166.6 0.6 copy-start.7

commit v2 on v1

--- a/solution.py
+++ b/solution.py
@@ -319,7 +319,7 @@
 MESH = pl.DeviceIdType.MESH
 BF = jnp.bfloat16
 F32 = jnp.float32
-QKV, OUT, UP, DOWN = range(4)
+QKV, OUT, UP, DOWN, SMALL = range(5)
 
 
 def dot_nn(a, b):
@@ -367,9 +367,9 @@
         "kf": ((tokens, local), BF),
         "vf": ((tokens, local), BF),
         "mask": ((batches, rows, rows), F32),
-        "car": ((batches, rows, local), F32),
-        "tail": ((batches, rows, local), F32),
-        "pmc": ((batches, rows, local), F32),
+        "car": ((batches, rows, 128), F32),
+        "tail": ((batches, rows, 128), F32),
+        "pmc": ((batches, rows, 128), F32),
         "low": ((batches, rows, heads * rows), BF),
         "numer": ((tokens, local), F32),
         "denom": ((tokens, local), F32),
@@ -394,19 +394,19 @@
         "gk": ((tokens, local), F32),
         "gv": ((tokens, local), F32),
         "gproj": ((3, tokens, local), BF),
-        "h_s1": ((4, 2, own, width), BF),
-        "h_r1": ((4, 2, own, width), BF),
-        "h_acc": ((4, 2, own, width), F32),
-        "h_s2": ((4, own, width), BF),
-        "h_r2": ((4, own, width), BF),
-        "rq_s": ((2, 2, hops, 3, block, local // 2), BF),
-        "rq_r": ((2, 2, hops, 3, block, local // 2), BF),
-        "ro_s": ((2, 2, hops, block, local // 2), BF),
-        "ro_r": ((2, 2, hops, block, local // 2), BF),
-        "ru_s": ((2, 2, hops, block, hidden // 2), BF),
-        "ru_r": ((2, 2, hops, block, hidden // 2), BF),
-        "rd_s": ((2, 2, hops, block, hidden // 2), BF),
-        "rd_r": ((2, 2, hops, block, hidden // 2), BF),
+        "h_s1": ((4, 2, 2, own // 2, width), BF),
+        "h_r1": ((4, 2, 2, own // 2, width), BF),
+        "h_acc": ((4, 2, 2, own // 2, width), F32),
+        "h_s2": ((4, 2, own // 2, width), BF),
+        "h_r2": ((4, 2, own // 2, width), BF),
+        "rq_s": ((n, 3, block, local), BF),
+        "rq_r": ((n, 3, block, local), BF),
+        "ro_s": ((n, block, local), BF),
+        "ro_r": ((n, block, local), BF),
+        "ru_s": ((n, block, hidden), BF),
+        "ru_r": ((n, block, hidden), BF),
+        "rd_s": ((n, block, hidden), BF),
+        "rd_r": ((n, block, hidden), BF),
         "fq": ((3, block, local), F32),
         "fo": ((block, local), F32),
         "fu": ((block, hidden), F32),
@@ -420,24 +420,22 @@
         "i_rows": ((own, width), F32),
     }
     sems = {
-        "ag_s": (4, 2, 2, hops),
-        "ag_r": (4, 2, 2, hops),
-        "rs_s": (4, 2, 2, hops),
-        "rs_r": (4, 2, 2, hops),
-        "hg_s": (4, 3),
-        "hg_r": (4, 3),
+        "ag_s": (5,),
+        "ag_r": (5, 2, hops),
+        "rs_s": (4,),
+        "rs_r": (4, 2, hops),
+        "hg_s": (4,),
+        "hg_r": (4, 2, 3),
         "hr_s": (4, 2),
-        "hr_r": (4, 2),
-        "st_s": (2, 2),
-        "st_r": (2, 2),
-        "sm_s": (n,),
-        "sm_r": (n,),
-        "aa_s": (2, m),
-        "aa_r": (2, m),
-        "hs_s": (m,),
-        "hs_r": (m,),
-        "ss_s": (n,),
-        "ss_r": (n,),
+        "hr_r": (4, 2, 2),
+        "st_s": (2,),
+        "st_r": (2,),
+        "aa_s": (2,),
+        "aa_r": (2,),
+        "hs_s": (1,),
+        "hs_r": (1,),
+        "ss_s": (1,),
+        "ss_r": (1,),
         "lc": (12,),
     }
     return vm, sems
@@ -485,11 +483,11 @@
             device_id_type=MESH,
         )
 
-    sent = []
-
-    def launch(copy):
-        copy.start()
-        sent.append(copy)
+    def drained(view, sem):
+        remote(view, view, sem, sem, ring[0], h).wait_send()
+
+    def landed(view, sem):
+        remote(view, view, sem, sem, ring[0], h).wait_recv()
 
     r.small[...] = jnp.zeros_like(r.small)
     r.small[0:2, :] = r.gains[...].astype(F32)
@@ -497,130 +495,129 @@
     r.small[5:6, :] = r.up_bias[...].astype(F32)
 
     barrier = pltpu.get_barrier_semaphore()
-    for i in range(1, n):
-        pl.semaphore_signal(
-            barrier, inc=1, device_id=(lax.rem(s + i, n), h), device_id_type=MESH
-        )
-    for i in range(1, m):
-        pl.semaphore_signal(
-            barrier, inc=1, device_id=(s, lax.rem(h + i, m)), device_id_type=MESH
-        )
-    pl.semaphore_wait(barrier, n - 1 + m - 1)
-
-    shards = (r.w_qkv, r.w_out, r.w_up, r.w_down)
-    gathered = (r.wq, r.wo, r.wu, r.wd)
-
-    def shard_piece(w, piece):
-        half = shards[w].shape[-1] // 2
-        cols = pl.ds(piece * half, half)
+    for peer in ((ring[0], h), (ring[1], h), (s, pair), (s, cross)):
+        pl.semaphore_signal(barrier, inc=1, device_id=peer, device_id_type=MESH)
+    pl.semaphore_wait(barrier, 4)
+
+    shards = (r.w_qkv, r.w_out, r.w_up, r.w_down, r.small)
+    gathered = (r.wq, r.wo, r.wu, r.wd, r.smallg)
+
+    def part_of(w, d, j):
+        wide_part = r.wq.shape[2] if w == QKV else shards[w].shape[1]
+        if j < hops - 1 or w == SMALL:
+            return pl.ds(0, wide_part)
+        return pl.ds(d * (wide_part // 2), wide_part // 2)
+
+    def ag_shard(w, d, j):
+        cols = part_of(w, d, j)
+        if w == SMALL:
+            return r.small
         return shards[w].at[:, :, cols] if w == QKV else shards[w].at[:, cols]
 
-    def full_piece(w, owner, piece):
-        half = gathered[w].shape[-1] // 2
-        cols = pl.ds(piece * half, half)
+    def ag_full(w, owner, d, j):
+        cols = part_of(w, d, j)
+        if w == SMALL:
+            return r.smallg.at[:, ds(owner * block, block)]
         if w == QKV:
-            return gathered[w].at[:, ds(owner * block, block), cols]
+            return r.wq.at[:, ds(owner * block, block), cols]
         return gathered[w].at[ds(owner * block, block), cols]
 
-    def lanes():
-        return [(piece, d) for piece in (0, 1) for d in (0, 1)]
-
-    def reach(piece, d):
-        return hops if piece == d else hops - 1
+    def ways(w, j):
+        return (0,) if w == SMALL and j == hops - 1 else (0, 1)
 
     def ag_send(w, j):
-        for piece, d in lanes():
-            if j < reach(piece, d):
-                owner = at(p - sign[d] * j)
-                src = shard_piece(w, piece) if j == 0 else full_piece(w, owner, piece)
-                launch(
-                    remote(
-                        src,
-                        full_piece(w, owner, piece),
-                        r.ag_s.at[w, piece, d, j],
-                        r.ag_r.at[w, piece, d, j],
-                        ring[d],
-                        h,
-                    )
-                )
+        for d in ways(w, j):
+            owner = at(p - sign[d] * j)
+            src = ag_shard(w, d, j) if j == 0 else ag_full(w, owner, d, j)
+            remote(
+                src, ag_full(w, owner, d, j), r.ag_s.at[w], r.ag_r.at[w, d, j], ring[d], h
+            ).start()
 
     def ag_wait(w, j):
-        for piece, d in lanes():
-            if j < reach(piece, d):
-                view = full_piece(w, at(p - sign[d] * (j + 1)), piece)
-                remote(
-                    view, view, r.ag_s.at[w, piece, d, j], r.ag_r.at[w, piece, d, j], ring[d], h
-                ).wait_recv()
+        for d in ways(w, j):
+            landed(ag_full(w, at(p - sign[d] * (j + 1)), d, j), r.ag_r.at[w, d, j])
 
     def ag_pass(w, j):
         ag_wait(w, j)
         ag_send(w, j + 1)
 
-    def hg_view(k, who):
+    part_rows = own // 2
+
+    def hg_view(k, c, who):
         if k < 2:
-            return (r.xg, r.cg)[k].at[:, :, ds(who * local, local)]
-        return (r.ntwo, r.gatt)[k - 2].at[ds(who * own, own), :]
-
-    def hg_copy(k, i, src, who, to):
-        return remote(src, hg_view(k, who), r.hg_s.at[k, i], r.hg_r.at[k, i], s, to)
-
-    def hg_start(k, src):
-        launch(hg_copy(k, 1, src, h, cross))
-        launch(hg_copy(k, 0, src, h, pair))
-
-    def hg_forward(k):
-        view = hg_view(k, cross)
-        hg_copy(k, 1, view, cross, cross).wait_recv()
-        launch(hg_copy(k, 2, view, cross, pair))
-
-    def hg_finish(k):
-        view = hg_view(k, pair)
-        hg_copy(k, 0, view, pair, pair).wait_recv()
+            return (r.xg, r.cg)[k].at[c, :, ds(who * local, local)]
+        return (r.ntwo, r.gatt)[k - 2].at[ds(who * own + c * part_rows, part_rows), :]
+
+    def hg_copy(k, c, i, src, who, to):
+        return remote(src, hg_view(k, c, who), r.hg_s.at[k], r.hg_r.at[k, c, i], s, to)
+
+    def hg_start(k, c):
+        src = (r.tok, r.cot)[k].at[c] if k < 2 else hg_view(k, c, h)
+        hg_copy(k, c, 1, src, h, cross).start()
+        hg_copy(k, c, 0, src, h, pair).start()
+
+    def hg_forward(k, c):
+        view = hg_view(k, c, cross)
+        hg_copy(k, c, 1, view, cross, cross).wait_recv()
+        hg_copy(k, c, 2, view, cross, pair).start()
+
+    def hg_finish(k, c):
+        view = hg_view(k, c, pair)
+        hg_copy(k, c, 0, view, pair, pair).wait_recv()
         across = lax.rem(pair + 2, m)
-        view = hg_view(k, across)
-        hg_copy(k, 2, view, across, pair).wait_recv()
-
-    def hr_rows(who):
-        return ds(who * own, own)
-
-    def hr_first(k, term):
-        for q in (0, 1):
-            who = 2 * q + 1 - lo
-            term(hr_rows(who), lambda cols, v, q=q: put(r.h_s1.at[k, q], cols, v))
-        launch(remote(r.h_s1.at[k], r.h_r1.at[k], r.hr_s.at[k, 0], r.hr_r.at[k, 0], s, pair))
-        for q in (0, 1):
-            who = 2 * q + lo
-            term(hr_rows(who), lambda cols, v, q=q: put(r.h_acc.at[k, q], cols, v))
-
-    def put(ref, cols, value):
-        ref[:, cols] = value.astype(ref.dtype)
-
-    def hr_second(k):
-        remote(
-            r.h_s1.at[k], r.h_r1.at[k], r.hr_s.at[k, 0], r.hr_r.at[k, 0], s, pair
-        ).wait_recv()
-        tile = 32
+        view = hg_view(k, c, across)
+        hg_copy(k, c, 2, view, across, pair).wait_recv()
+
+    tn = 256
+
+    def hr_first(k, c, left, product):
+        blocks = [2 * i + 1 - lo for i in (0, 1)] + [2 * i + lo for i in (0, 1)]
+        where = [ds(who * own + c * part_rows, part_rows) for who in blocks]
+
+        def some(i):
+            cols = ds(i * tn, tn)
+            v = product(left(where), cols)
+            for q in (0, 1):
+                r.h_s1[k, c, q, :, cols] = v[q * part_rows : (q + 1) * part_rows].astype(BF)
+                r.h_acc[k, c, q, :, cols] = v[(q + 2) * part_rows : (q + 3) * part_rows]
+
+        loop(width // tn, some)
+        hr_copy(k, c, 0).start()
+
+    def hr_copy(k, c, stage):
+        if stage == 0:
+            src, dst, to = r.h_s1.at[k, c], r.h_r1.at[k, c], pair
+        else:
+            src, dst, to = r.h_s2.at[k, c], r.h_r2.at[k, c], cross
+        return remote(src, dst, r.hr_s.at[k, stage], r.hr_r.at[k, c, stage], s, to)
+
+    def hr_second(k, c):
+        hr_copy(k, c, 0).wait_recv()
 
         def away(i):
-            rw = ds(i * tile, tile)
-            r.h_s2[k, rw, :] = (
-                r.h_acc[k, 1 - hi, rw, :] + r.h_r1[k, 1 - hi, rw, :].astype(F32)
+            rw = ds(i * 32, 32)
+            r.h_s2[k, c, rw, :] = (
+                r.h_acc[k, c, 1 - hi, rw, :] + r.h_r1[k, c, 1 - hi, rw, :].astype(F32)
             ).astype(BF)
 
-        loop(own // tile, away)
-        launch(remote(r.h_s2.at[k], r.h_r2.at[k], r.hr_s.at[k, 1], r.hr_r.at[k, 1], s, cross))
-
-    def hr_wait(k):
-        remote(
-            r.h_s2.at[k], r.h_r2.at[k], r.hr_s.at[k, 1], r.hr_r.at[k, 1], s, cross
-        ).wait_recv()
-
-    def hr_value(k, rw):
+        loop(part_rows // 32, away)
+        hr_copy(k, c, 1).start()
+
+    def hr_wait(k, c):
+        hr_copy(k, c, 1).wait_recv()
+
+    def hr_value(k, c, rw):
         return (
-            r.h_acc[k, hi, rw, :]
-            + r.h_r1[k, hi, rw, :].astype(F32)
-            + r.h_r2[k, rw, :].astype(F32)
-        )
+            r.h_acc[k, c, hi, rw, :]
+            + r.h_r1[k, c, hi, rw, :].astype(F32)
+            + r.h_r2[k, c, rw, :].astype(F32)
+        )
+
+    def pick(ref):
+        return lambda where: jnp.concatenate([ref[rw, :] for rw in where], axis=0)
+
+    def product_nt(right):
+        return lambda left, cols: dot_nt(left, right[cols, :])
 
     def rs_term(w, owner, piece):
         cols = ds(owner * block, block)
@@ -640,57 +637,59 @@
     rs_send = (r.rq_s, r.ro_s, r.ru_s, r.rd_s)
     rs_recv = (r.rq_r, r.ro_r, r.ru_r, r.rd_r)
 
-    def rs_copy(w, piece, d, j):
-        return remote(
-            rs_send[w].at[piece, d, j],
-            rs_recv[w].at[piece, d, j],
-            r.rs_s.at[w, piece, d, j],
-            r.rs_r.at[w, piece, d, j],
-            ring[d],
-            h,
-        )
+    def rs_half(w, piece):
+        half = rs_send[w].shape[-1] // 2
+        return pl.ds(piece * half, half)
+
+    def rs_view(ref, w, d, step):
+        if step > 0:
+            return ref.at[d * hops + step]
+        if w == QKV:
+            return ref.at[d * hops, :, :, rs_half(w, d)]
+        return ref.at[d * hops, :, rs_half(w, d)]
+
+    def rs_arrived(w, d, step):
+        landed(rs_view(rs_recv[w], w, d, step), r.rs_r.at[w, d, step])
 
     def rs_round(w, step):
-        waiting = None
-        for piece, d in lanes():
-            far = reach(piece, d)
-            j = step - (hops - far)
-            if j < 0:
-                continue
-            terms = rs_term(w, at(p + sign[d] * (far - j)), piece)
-            if j > 0:
-                rs_copy(w, piece, d, j - 1).wait_recv()
-            for i, v in enumerate(terms):
-                where = (piece, d, j, i) if w == QKV else (piece, d, j)
-                before = (piece, d, j - 1, i) if w == QKV else (piece, d, j - 1)
-                if j > 0:
-                    v = v + rs_recv[w][before].astype(F32)
-                rs_send[w][where] = v.astype(BF)
-            if waiting is not None:
-                launch(waiting)
-            waiting = rs_copy(w, piece, d, j)
-        launch(waiting)
+        for d in (0, 1):
+            slot = d * hops + step
+            if step > 0:
+                rs_arrived(w, d, step - 1)
+            for piece in (0, 1):
+                if step == 0 and piece != d:
+                    continue
+                terms = rs_term(w, at(p + sign[d] * (hops - step)), piece)
+                cols = rs_half(w, piece)
+                for i, v in enumerate(terms):
+                    lead = (i,) if w == QKV else ()
+                    if step > 1 or (step == 1 and piece == d):
+                        v = v + rs_recv[w][(slot - 1, *lead, slice(None), cols)].astype(F32)
+                    rs_send[w][(slot, *lead, slice(None), cols)] = v.astype(BF)
+            remote(
+                rs_view(rs_send[w], w, d, step),
+                rs_view(rs_recv[w], w, d, step),
+                r.rs_s.at[w],
+                r.rs_r.at[w, d, step],
+                ring[d],
+                h,
+            ).start()
 
     finals = (r.fq, r.fo, r.fu, r.fd)
     results = (r.gq_o, r.go_o, r.gu_o, r.gd_o)
     local_copies = []
 
     def rs_final(w):
+        terms = [rs_term(w, s, piece) for piece in (0, 1)]
+        for d in (0, 1):
+            rs_arrived(w, d, hops - 1)
         for piece in (0, 1):
-            terms = rs_term(w, s, piece)
-            for d in (0, 1):
-                rs_copy(w, piece, d, reach(piece, d) - 1).wait_recv()
-            half = finals[w].shape[-1] // 2
-            cols = pl.ds(piece * half, half)
-            for i, v in enumerate(terms):
+            cols = rs_half(w, piece)
+            for i, v in enumerate(terms[piece]):
+                lead = (i,) if w == QKV else ()
                 for d in (0, 1):
-                    j = reach(piece, d) - 1
-                    where = (piece, d, j, i) if w == QKV else (piece, d, j)
-                    v = v + rs_recv[w][where].astype(F32)
-                if w == QKV:
-                    finals[w][i, :, cols] = v
-                else:
-                    finals[w][:, cols] = v
+                    v = v + rs_recv[w][(d * hops + hops - 1, *lead, slice(None), cols)].astype(F32)
+                finals[w][(*lead, slice(None), cols)] = v
         copy = pltpu.make_async_copy(finals[w], results[w], r.lc.at[w])
         copy.start()
         local_copies.append(copy)
@@ -699,71 +698,53 @@
         where = (hi, ds(lo * own, own))
         for i in range(1, m):
             to = lax.rem(h + i, m)
-            launch(
-                remote(
-                    src.at[:, ds(to * local, local)],
-                    dst.at[where[0], where[1], :],
-                    r.aa_s.at[k, i],
-                    r.aa_r.at[k, i],
-                    s,
-                    to,
-                )
-            )
+            remote(
+                src.at[:, ds(to * local, local)],
+                dst.at[where[0], where[1], :],
+                r.aa_s.at[k],
+                r.aa_r.at[k],
+                s,
+                to,
+            ).start()
         copy = pltpu.make_async_copy(
             src.at[:, ds(h * local, local)], dst.at[where[0], where[1], :], r.lc.at[4 + k]
         )
         copy.start()
         local_copies.append(copy)
 
-    def turn_wait(k, src, dst):
-        for i in range(1, m):
-            who = lax.rem(h + m - i, m)
-            remote(
-                src.at[:, ds(h * local, local)],
-                dst.at[lax.div(who, 2), ds(lax.rem(who, 2) * own, own), :],
-                r.aa_s.at[k, i],
-                r.aa_r.at[k, i],
-                s,
-                who,
-            ).wait_recv()
-
+    def turn_wait(k, src):
+        landed(src.at[:, pl.ds(0, (m - 1) * local)], r.aa_r.at[k])
+
+    ag_send(SMALL, 0)
     ag_send(QKV, 0)
     ag_send(OUT, 0)
-    hg_start(0, r.tok)
-    for i in range(1, n):
-        to = lax.rem(s + i, n)
-        launch(
-            remote(
-                r.small,
-                r.smallg.at[:, ds(s * block, block)],
-                r.sm_s.at[i],
-                r.sm_r.at[i],
-                to,
-                h,
-            )
-        )
+    hg_start(0, 0)
+    hg_start(0, 1)
     own_copies = [
-        pltpu.make_async_copy(r.tok, hg_view(0, h), r.lc.at[6]),
-        pltpu.make_async_copy(r.cot, hg_view(1, h), r.lc.at[7]),
         pltpu.make_async_copy(r.w_qkv, r.wq.at[:, ds(s * block, block), :], r.lc.at[8]),
         pltpu.make_async_copy(r.w_out, r.wo.at[ds(s * block, block), :], r.lc.at[9]),
         pltpu.make_async_copy(r.w_up, r.wu.at[ds(s * block, block), :], r.lc.at[10]),
         pltpu.make_async_copy(r.w_down, r.wd.at[ds(s * block, block), :], r.lc.at[11]),
+        pltpu.make_async_copy(r.tok, r.xg.at[:, :, ds(h * local, local)], r.lc.at[6]),
+        pltpu.make_async_copy(r.cot, r.cg.at[:, :, ds(h * local, local)], r.lc.at[7]),
     ]
     for copy in own_copies:
         copy.start()
-    hg_start(1, r.cot)
+    hg_start(1, 0)
+    hg_start(1, 1)
 
     first = s * rows
-    row_at = lax.broadcasted_iota(jnp.int32, (rows, local), 0)
+    row_at = lax.broadcasted_iota(jnp.int32, (rows, 128), 0)
     lane_at = lax.broadcasted_iota(jnp.int32, (rows, rows), 1)
     square = lax.broadcasted_iota(jnp.int32, (local, local), 0)
     square_lane = lax.broadcasted_iota(jnp.int32, (local, local), 1)
     same_head = (square // DH) == (square_lane // DH)
     diagonal = square == square_lane
-    ones = jnp.ones((rows, local), BF)
     lane_head = lax.broadcasted_iota(jnp.int32, (rows, local), 1) // DH
     before_thr, after_thr = [], []
+
+    def wide(value):
+        return jnp.concatenate([value] * (local // 128), axis=1)
 
     def begin(offsets, place):
         value = 0
@@ -776,46 +757,39 @@
             begin(offsets, which * rows + rows - 1) < which * rows, 1.0, 0.0
         ).astype(F32)
 
-    for b in range(batches):
+    def crops(b):
         offsets, running = [], 0
         for i in range(r.lengths.shape[1]):
             offsets.append(running)
             running = running + r.lengths[b, i]
-        start = jnp.zeros((rows, local), jnp.int32)
+        start = jnp.zeros((rows, 128), jnp.int32)
         for off in offsets:
             start = jnp.where(off <= row_at + first, off, start)
         last = begin(offsets, first + rows - 1)
         r.mask[b] = jnp.where(
-            (lane_at + first >= start) & (lane_at <= row_at), 1.0, 0.0
+            (lane_at + first >= wide(start)) & (lane_at <= wide(row_at)), 1.0, 0.0
         ).astype(F32)
         r.car[b] = jnp.where(start < first, 1.0, 0.0).astype(F32)
         r.tail[b] = jnp.where(start == last, 1.0, 0.0).astype(F32)
         before_thr.append(through(offsets, lax.rem(s + n - 1, n)))
         after_thr.append(through(offsets, lax.rem(s + 1, n)))
         keep = r.pixel[b : b + 1, :].astype(F32)
-        r.pmc[b] = dot_nn(jnp.where(diagonal, keep, 0.0).astype(BF), ones)
-
-    ag_pass(QKV, 0)
-    ag_pass(OUT, 0)
-    hg_forward(0)
-
-    for i in range(1, n):
-        who = lax.rem(s + n - i, n)
-        remote(
-            r.small,
-            r.smallg.at[:, ds(who * block, block)],
-            r.sm_s.at[i],
-            r.sm_r.at[i],
-            who,
-            h,
-        ).wait_recv()
-    r.smallg[:, ds(s * block, block)] = r.small[...]
+        r.pmc[b] = dot_nn(
+            jnp.where(diagonal, keep, 0.0).astype(BF), jnp.ones((rows, 128), BF)
+        )
+
+    def ag_step(j):
+        ag_pass(SMALL, j)
+        ag_pass(QKV, j)
+        ag_pass(OUT, j)
+
+    crops(0)
+    for c in (0, 1):
+        hg_forward(0, c)
+    ag_step(0)
     for copy in own_copies:
         copy.wait()
-    hg_finish(0)
-    gain_one, gain_two = r.smallg[0:1, :], r.smallg[1:2, :]
-    shift_one, shift_two, shift_out = r.smallg[2:3, :], r.smallg[3:4, :], r.smallg[4:5, :]
-    up_shift = r.smallg[5:6, :]
+    r.smallg[:, ds(s * block, block)] = r.small[...]
 
     def unit(values):
         mean = jnp.mean(values, axis=1, keepdims=True)
@@ -825,21 +799,31 @@
 
     tile = 32
 
+    def unit_one(b):
+        def some(i):
+            u, _ = unit(r.xg[b, ds(i * tile, tile), :].astype(F32))
+            r.gelu_d[ds(b * rows + i * tile, tile), :] = u
+
+        loop(rows // tile, some)
+
     def norm_one(i):
-        b = lax.div(i, rows // tile)
-        rw = ds(lax.rem(i, rows // tile) * tile, tile)
-        u, _ = unit(r.xg[b, rw, :].astype(F32))
-        r.normed[ds(i * tile, tile), :] = (u * gain_one + shift_one).astype(BF)
-
-    ag_pass(QKV, 1)
-    ag_pass(OUT, 1)
+        rw = ds(i * tile, tile)
+        r.normed[rw, :] = (r.gelu_d[rw, :] * gain_one + shift_one).astype(BF)
+
+    for c in (0, 1):
+        hg_finish(0, c)
+    unit_one(0)
+    ag_step(1)
+    unit_one(1)
+    crops(1)
+    ag_step(2)
+    ag_send(UP, 0)
+    for c in (0, 1):
+        hg_forward(1, c)
+    ag_wait(SMALL, 3)
+    gain_one, gain_two = r.smallg[0:1, :], r.smallg[1:2, :]
+    shift_one, shift_two, shift_out = r.smallg[2:3, :], r.smallg[3:4, :], r.smallg[4:5, :]
     loop(tokens // tile, norm_one)
-    hg_forward(1)
-    ag_pass(QKV, 2)
-    ag_pass(OUT, 2)
-    ag_send(UP, 0)
-    ag_send(DOWN, 0)
-    hg_finish(1)
     ag_wait(QKV, 3)
     ag_wait(OUT, 3)
 
@@ -858,7 +842,7 @@
             if kind == 0:
                 r.qf[rw, :] = f
             else:
-                r.kf[rw, :] = (f.astype(F32) * r.pmc[b, rb, :]).astype(BF)
+                r.kf[rw, :] = (f.astype(F32) * wide(r.pmc[b, rb, :])).astype(BF)
         r.vf[rw, :] = dot_nn(left, r.wq[2]).astype(BF)
 
     loop(tokens // tm, project)
@@ -879,12 +863,10 @@
     def state_send(k, ref, dest, step):
         for i in (0, 1):
             to = lax.rem(s + n + step * (i + 1), n)
-            launch(remote(ref, dest.at[i], r.st_s.at[k, i], r.st_r.at[k, i], to, h))
-
-    def state_wait(k, ref, dest, step):
-        for i in (0, 1):
-            to = lax.rem(s + n + step * (i + 1), n)
-            remote(ref, dest.at[i], r.st_s.at[k, i], r.st_r.at[k, i], to, h).wait_recv()
+            remote(ref, dest.at[i], r.st_s.at[k], r.st_r.at[k], to, h).start()
+
+    def state_wait(k, dest):
+        landed(dest, r.st_r.at[k])
 
     def rows_of(b):
         return pl.ds(b * rows, rows)
@@ -896,7 +878,7 @@
         )
 
     for b in range(batches):
-        k = r.kf[rows_of(b), :].astype(F32) * r.tail[b]
+        k = r.kf[rows_of(b), :].astype(F32) * wide(r.tail[b])
         moved = dot_tn(k.astype(BF), r.vf[rows_of(b), :])
         a, t = fold(moved, jnp.sum(k, axis=0, keepdims=True))
         r.st_send[b, 0:DH, :] = a
@@ -913,12 +895,14 @@
         r.denom[rows_of(b), :] = acc
         r.numer[rows_of(b), :] = dot_nn(r.low[b], by_head(r.vf[rows_of(b), :]))
 
+    for c in (0, 1):
+        hg_finish(1, c)
     ag_pass(UP, 0)
-    ag_pass(DOWN, 0)
-    state_wait(0, r.st_send, r.st_recv, 1)
+    ag_send(DOWN, 0)
+    state_wait(0, r.st_recv)
 
     def both(b, value, thr):
-        one = value.astype(F32) * r.car[b]
+        one = value.astype(F32) * wide(r.car[b])
         return jnp.concatenate([one.astype(BF), (one * thr).astype(BF)], axis=1)
 
     for b in range(batches):
@@ -942,77 +926,75 @@
         r.denom[rows_of(b), :] = bottom
         r.mixed[rows_of(b), :] = attn.astype(BF)
 
-    tn = 256
-
-    def product_nt(left_ref, right_ref):
-        def term(rw, store):
-            def part(i):
-                cols = ds(i * tn, tn)
-                store(cols, dot_nt(left_ref[rw, :], right_ref[cols, :]))
-
-            loop(width // tn, part)
-
-        return term
-
-    hr_first(0, product_nt(r.mixed, r.wo))
-    hr_second(0)
+    hr_first(0, 0, pick(r.mixed), product_nt(r.wo))
+    hr_first(0, 1, pick(r.mixed), product_nt(r.wo))
+    hr_second(0, 0)
+    hr_second(0, 1)
     ag_pass(UP, 1)
+    mine = h * own
+
+    def x_rows(at_row):
+        return r.xg[hi, ds(lo * own + at_row, tile), :].astype(F32)
+
+    def c_rows(at_row):
+        return r.cg[hi, ds(lo * own + at_row, tile), :].astype(F32)
+
+    def norm_two(c):
+        def some(i):
+            at_row = c * part_rows + i * tile
+            v = x_rows(at_row) + hr_value(0, c, ds(i * tile, tile))
+            r.middle[ds(at_row, tile), :] = v
+            u, _ = unit(v)
+            r.ntwo[ds(mine + at_row, tile), :] = (u * gain_two + shift_two).astype(BF)
+
+        loop(part_rows // tile, some)
+
+    for c in (0, 1):
+        hr_wait(0, c)
+        norm_two(c)
+        hg_start(2, c)
+    ag_pass(DOWN, 0)
+    hg_forward(2, 0)
+    hg_forward(2, 1)
+    ag_pass(UP, 2)
+    hg_finish(2, 0)
+    hg_finish(2, 1)
     ag_pass(DOWN, 1)
-    hr_wait(0)
-    mine = h * own
-
-    def x_rows(i):
-        return r.xg[hi, ds(lo * own + i * tile, tile), :].astype(F32)
-
-    def c_rows(i):
-        return r.cg[hi, ds(lo * own + i * tile, tile), :].astype(F32)
-
-    def norm_two(i):
-        rw = ds(i * tile, tile)
-        v = x_rows(i) + hr_value(0, rw)
-        r.middle[rw, :] = v
-        u, _ = unit(v)
-        r.ntwo[ds(mine + i * tile, tile), :] = (u * gain_two + shift_two).astype(BF)
-
-    loop(own // tile, norm_two)
-    hg_start(2, hg_view(2, h))
-    ag_pass(UP, 2)
+    ag_wait(UP, 3)
+
+    tu = 256
+
+    def up(i):
+        rw = ds(lax.div(i, hidden // tn) * tu, tu)
+        cols = ds(lax.rem(i, hidden // tn) * tn, tn)
+        v = dot_nn(r.ntwo[rw, :], r.wu[:, cols]) + r.smallg[5:6, cols]
+        square_of = v * v
+        t = jnp.tanh(0.7978845608028654 * (v + 0.044715 * (square_of * v)))
+        half = 0.5 * (1.0 + t)
+        r.activ[rw, cols] = (v * half).astype(BF)
+        r.gelu_d[rw, cols] = half + (0.5 * v) * (1.0 - t * t) * (
+            0.7978845608028654 + (3.0 * 0.044715 * 0.7978845608028654) * square_of
+        )
+
+    loop((tokens // tu) * (hidden // tn), up)
+    rs_round(DOWN, 0)
     ag_pass(DOWN, 2)
-    hg_forward(2)
-    hg_finish(2)
-    ag_wait(UP, 3)
-
-    ft = 256
-
-    def up(i):
-        rw = ds(lax.div(i, hidden // ft) * tm, tm)
-        cols = ds(lax.rem(i, hidden // ft) * ft, ft)
-        v = dot_nn(r.ntwo[rw, :], r.wu[:, cols]) + r.smallg[5:6, cols]
-        cube = 0.7978845608028654 * (v + 0.044715 * (v * v * v))
-        t = jnp.tanh(cube)
-        r.activ[rw, cols] = (0.5 * v * (1.0 + t)).astype(BF)
-        r.gelu_d[rw, cols] = 0.5 * (1.0 + t) + 0.5 * v * (1.0 - t * t) * (
-            0.7978845608028654 * (1.0 + 3.0 * 0.044715 * (v * v))
-        )
-
-    loop((tokens // tm) * (hidden // ft), up)
-    rs_round(DOWN, 0)
     ag_wait(DOWN, 3)
 
     def back(i):
-        rw = ds(lax.div(i, hidden // ft) * tm, tm)
-        cols = ds(lax.rem(i, hidden // ft) * ft, ft)
-        b = lax.div(lax.div(i, hidden // ft), rows // tm)
-        rb = ds(lax.rem(lax.div(i, hidden // ft), rows // tm) * tm, tm)
-        g = dot_nn(r.cg[b, rb, :], r.wd[:, cols])
-        r.g_hid[rw, cols] = (g * r.gelu_d[rw, cols]).astype(BF)
-
-    loop((tokens // tm) * (hidden // ft), back)
-    hr_first(2, product_nt(r.g_hid, r.wu))
-    hr_second(2)
+        cols = ds(i * tn, tn)
+        for b in range(batches):
+            g = dot_nn(r.cg[b], r.wd[:, cols])
+            r.g_hid[rows_of(b), cols] = (g * r.gelu_d[rows_of(b), cols]).astype(BF)
+
+    loop(hidden // tn, back)
     rs_round(UP, 0)
+    hr_first(2, 0, pick(r.g_hid), product_nt(r.wu))
+    hr_first(2, 1, pick(r.g_hid), product_nt(r.wu))
     rs_round(DOWN, 1)
-    hr_wait(2)
+    hr_second(2, 0)
+    hr_second(2, 1)
+    rs_round(UP, 1)
 
     r.hs_send[...] = jnp.zeros_like(r.hs_send)
 
@@ -1021,26 +1003,31 @@
         centered = scaled - jnp.mean(scaled, axis=1, keepdims=True)
         return inverse * (centered - u * jnp.mean(scaled * u, axis=1, keepdims=True))
 
-    def norm_two_back(i):
-        rw = ds(i * tile, tile)
-        g = hr_value(2, rw)
-        u, inverse = unit(r.middle[rw, :])
-        out = c_rows(i)
-        v = out + back_norm(g, u, inverse, gain_two)
-        r.g_mid[rw, :] = v
-        r.gatt[ds(mine + i * tile, tile), :] = v.astype(BF)
-        r.hs_send[1:2, :] += jnp.sum(g * u, axis=0, keepdims=True)
-        r.hs_send[3:4, :] += jnp.sum(g, axis=0, keepdims=True)
-        r.hs_send[4:5, :] += jnp.sum(out, axis=0, keepdims=True)
-
-    loop(own // tile, norm_two_back)
-    hg_start(3, hg_view(3, h))
-    hr_first(1, product_nt(r.activ, r.wd))
-    rs_round(UP, 1)
-    hg_forward(3)
-    hr_second(1)
+    def norm_two_back(c):
+        def some(i):
+            at_row = c * part_rows + i * tile
+            rw = ds(at_row, tile)
+            g = hr_value(2, c, ds(i * tile, tile))
+            u, inverse = unit(r.middle[rw, :])
+            out = c_rows(at_row)
+            v = out + back_norm(g, u, inverse, gain_two)
+            r.g_mid[rw, :] = v
+            r.gatt[ds(mine + at_row, tile), :] = v.astype(BF)
+            r.hs_send[1:2, :] += jnp.sum(g * u, axis=0, keepdims=True)
+            r.hs_send[3:4, :] += jnp.sum(g, axis=0, keepdims=True)
+            r.hs_send[4:5, :] += jnp.sum(out, axis=0, keepdims=True)
+
+        loop(part_rows // tile, some)
+
+    for c in (0, 1):
+        hr_wait(2, c)
+        norm_two_back(c)
+        hg_start(3, c)
     rs_round(DOWN, 2)
-    hg_finish(3)
+    for c in (0, 1):
+        hg_forward(3, c)
+    for c in (0, 1):
+        hg_finish(3, c)
 
     def mixed_back(i):
         rw = ds(i * tm, tm)
@@ -1061,13 +1048,13 @@
     loop(tokens // tm, mixed_back)
 
     for b in range(batches):
-        q = r.qf[rows_of(b), :].astype(F32) * r.car[b]
+        q = r.qf[rows_of(b), :].astype(F32) * wide(r.car[b])
         moved = dot_tn(q.astype(BF), r.g_num[rows_of(b), :])
         a, t = fold(moved, jnp.sum(q * r.g_den[rows_of(b), :], axis=0, keepdims=True))
         r.gs_send[b, 0:DH, :] = a
         r.gs_send[b, DH:, :] = t
     state_send(1, r.gs_send, r.gs_recv, -1)
-    rs_round(OUT, 0)
+    rs_round(UP, 2)
 
     def head_lanes(hd, value):
         return jnp.where(lane_head == hd, value.astype(F32), 0.0).astype(BF)
@@ -1090,14 +1077,13 @@
             r.st_recv[0, b, DH : DH + 16, :].astype(F32)[0:1]
             + before_thr[b] * r.st_recv[1, b, DH : DH + 16, :].astype(F32)[0:1]
         )
-        gq = gq + dot_nt(left, states) + r.car[b] * r.g_den[rw, :] * totals
+        gq = gq + dot_nt(left, states) + wide(r.car[b]) * r.g_den[rw, :] * totals
         r.gproj[0, rw, :] = (gq * r.phi_d[0, rw, :]).astype(BF)
         r.gk[rw, :] = gk
         r.gv[rw, :] = gv
 
-    rs_round(OUT, 1)
-    rs_round(UP, 2)
-    state_wait(1, r.gs_send, r.gs_recv, -1)
+    rs_round(OUT, 0)
+    state_wait(1, r.gs_recv)
     for b in range(batches):
         rw = rows_of(b)
         thr = after_thr[b]
@@ -1106,60 +1092,77 @@
             r.gs_recv[0, b, DH : DH + 16, :].astype(F32)[0:1]
             + thr * r.gs_recv[1, b, DH : DH + 16, :].astype(F32)[0:1]
         )
-        k = r.kf[rw, :].astype(F32) * r.tail[b]
-        v = r.vf[rw, :].astype(F32) * r.tail[b]
+        k = r.kf[rw, :].astype(F32) * wide(r.tail[b])
+        v = r.vf[rw, :].astype(F32) * wide(r.tail[b])
         k2 = jnp.concatenate([k.astype(BF), (k * thr).astype(BF)], axis=1)
         v2 = jnp.concatenate([v.astype(BF), (v * thr).astype(BF)], axis=1)
-        gk = r.gk[rw, :] + dot_nt(v2, jnp.concatenate(states, axis=1)) + r.tail[b] * totals
+        gk = r.gk[rw, :] + dot_nt(v2, jnp.concatenate(states, axis=1)) + wide(r.tail[b]) * totals
         gv = r.gv[rw, :] + dot_nn(k2, jnp.concatenate(states, axis=0))
-        r.gproj[1, rw, :] = (gk * r.pmc[b] * r.phi_d[1, rw, :]).astype(BF)
+        r.gproj[1, rw, :] = (gk * wide(r.pmc[b]) * r.phi_d[1, rw, :]).astype(BF)
         r.gproj[2, rw, :] = gv.astype(BF)
 
-    def first_term(rw, store):
-        def part(i):
-            cols = ds(i * tn, tn)
-            v = dot_nt(r.gproj[0, rw, :], r.wq[0, cols, :])
-            for kind in (1, 2):
-                v = v + dot_nt(r.gproj[kind, rw, :], r.wq[kind, cols, :])
-            store(cols, v)
-
-        loop(width // tn, part)
-
-    hr_first(3, first_term)
-    hr_second(3)
     rs_round(QKV, 0)
     rs_round(DOWN, 3)
+
+    def picks(where):
+        return [
+            jnp.concatenate([r.gproj[kind, rw, :] for rw in where], axis=0) for kind in range(3)
+        ]
+
+    def first_term(left, cols):
+        v = dot_nt(left[0], r.wq[0, cols, :])
+        for kind in (1, 2):
+            v = v + dot_nt(left[kind], r.wq[kind, cols, :])
+        return v
+
+    hr_first(3, 0, picks, first_term)
+    hr_first(3, 1, picks, first_term)
+    hr_second(3, 0)
+    hr_second(3, 1)
+    rs_round(QKV, 1)
+    rs_round(OUT, 1)
+    rs_round(UP, 3)
+    hr_first(1, 0, pick(r.activ), product_nt(r.wd))
+    hr_first(1, 1, pick(r.activ), product_nt(r.wd))
+    hr_second(1, 0)
+    hr_second(1, 1)
+
+    def norm_one_back(c):
+        def some(i):
+            at_row = c * part_rows + i * tile
+            rw = ds(at_row, tile)
+            g = hr_value(3, c, ds(i * tile, tile))
+            u, inverse = unit(x_rows(at_row))
+            r.i_rows[rw, :] = r.g_mid[rw, :] + back_norm(g, u, inverse, gain_one)
+            r.hs_send[0:1, :] += jnp.sum(g * u, axis=0, keepdims=True)
+            r.hs_send[2:3, :] += jnp.sum(g, axis=0, keepdims=True)
+
+        loop(part_rows // tile, some)
+
+    for c in (0, 1):
+        hr_wait(3, c)
+        norm_one_back(c)
+    turn(1, r.i_rows, r.ing_o)
     rs_round(OUT, 2)
-    rs_round(UP, 3)
-    rs_round(QKV, 1)
-
-    hr_wait(1)
-
-    def finish_rows(i):
-        rw = ds(i * tile, tile)
-        r.a_rows[rw, :] = r.middle[rw, :] + hr_value(1, rw) + shift_out
-
-    loop(own // tile, finish_rows)
+    rs_round(QKV, 2)
+
+    def finish_rows(c):
+        def some(i):
+            rw = ds(c * part_rows + i * tile, tile)
+            r.a_rows[rw, :] = r.middle[rw, :] + hr_value(1, c, ds(i * tile, tile)) + shift_out
+
+        loop(part_rows // tile, some)
+
+    for c in (0, 1):
+        hr_wait(1, c)
+        finish_rows(c)
     turn(0, r.a_rows, r.act_o)
-
-    hr_wait(3)
-
-    def norm_one_back(i):
-        rw = ds(i * tile, tile)
-        g = hr_value(3, rw)
-        u, inverse = unit(x_rows(i))
-        r.i_rows[rw, :] = r.g_mid[rw, :] + back_norm(g, u, inverse, gain_one)
-        r.hs_send[0:1, :] += jnp.sum(g * u, axis=0, keepdims=True)
-        r.hs_send[2:3, :] += jnp.sum(g, axis=0, keepdims=True)
-
-    loop(own // tile, norm_one_back)
-    turn(1, r.i_rows, r.ing_o)
 
     r.hs_recv[h] = r.hs_send[...]
     for i in range(1, m):
-        launch(
-            remote(r.hs_send, r.hs_recv.at[h], r.hs_s.at[i], r.hs_r.at[i], s, lax.rem(h + i, m))
-        )
+        remote(
+            r.hs_send, r.hs_recv.at[h], r.hs_s.at[0], r.hs_r.at[0], s, lax.rem(h + i, m)
+        ).start()
     r.upb[...] = jnp.zeros_like(r.upb)
 
     def column_sums(i):
@@ -1167,55 +1170,73 @@
 
     loop(tokens // tile, column_sums)
     rs_round(OUT, 3)
-    rs_round(QKV, 2)
-    for i in range(1, m):
-        who = lax.rem(h + m - i, m)
-        remote(r.hs_send, r.hs_recv.at[who], r.hs_s.at[i], r.hs_r.at[i], s, who).wait_recv()
+    rs_final(DOWN)
+    landed(r.hs_recv.at[pl.ds(0, m - 1)], r.hs_r.at[0])
     acc = r.hs_recv[0]
     for i in range(1, m):
         acc = acc + r.hs_recv[i]
     r.sg[...] = acc
     r.sg[5:6, :] = r.upb[...]
     r.ss_recv[s] = r.sg[:, ds(s * block, block)]
-    rs_final(DOWN)
     for i in range(1, n):
         to = lax.rem(s + i, n)
-        launch(
-            remote(
-                r.sg.at[:, ds(to * block, block)],
-                r.ss_recv.at[s],
-                r.ss_s.at[i],
-                r.ss_r.at[i],
-                to,
-                h,
-            )
-        )
+        remote(
+            r.sg.at[:, ds(to * block, block)],
+            r.ss_recv.at[s],
+            r.ss_s.at[0],
+            r.ss_r.at[0],
+            to,
+            h,
+        ).start()
+    rs_final(UP)
     rs_round(QKV, 3)
-    rs_final(UP)
     rs_final(OUT)
-    for i in range(1, n):
-        who = lax.rem(s + n - i, n)
-        remote(
-            r.sg.at[:, ds(s * block, block)],
-            r.ss_recv.at[who],
-            r.ss_s.at[i],
-            r.ss_r.at[i],
-            who,
-            h,
-        ).wait_recv()
+    landed(r.ss_recv.at[pl.ds(0, n - 1)], r.ss_r.at[0])
     acc = r.ss_recv[0]
     for i in range(1, n):
         acc = acc + r.ss_recv[i]
     r.gg_o[...] = acc[0:2]
     r.gb_o[...] = acc[2:5]
     r.gup_o[...] = acc[5:6]
+    turn_wait(0, r.a_rows)
+    turn_wait(1, r.i_rows)
+
+    far = pl.ds(0, (n - 1) * block)
+    for w in range(5):
+        views = (r.wq.at[:, far, :], r.wo.at[far], r.wu.at[far], r.wd.at[far], r.smallg.at[:, far])
+        drained(views[w], r.ag_s.at[w])
+    others = pl.ds(0, (m - 1) * local)
+    rest = pl.ds(0, (m - 1) * own)
+    for k in range(4):
+        view = (r.xg, r.cg)[k].at[:, :, others] if k < 2 else (r.ntwo, r.gatt)[k - 2].at[rest]
+        drained(view, r.hg_s.at[k])
+        drained(r.h_s1.at[k], r.hr_s.at[k, 0])
+        drained(r.h_s2.at[k], r.hr_s.at[k, 1])
+    for k, dest in enumerate((r.st_recv, r.gs_recv)):
+        drained(dest, r.st_s.at[k])
+    drained(r.a_rows.at[:, others], r.aa_s.at[0])
+    drained(r.i_rows.at[:, others], r.aa_s.at[1])
+    drained(r.hs_recv.at[pl.ds(0, m - 1)], r.hs_s.at[0])
+    drained(r.ss_recv.at[pl.ds(0, n - 1)], r.ss_s.at[0])
     rs_final(QKV)
-    turn_wait(0, r.a_rows, r.act_o)
-    turn_wait(1, r.i_rows, r.ing_o)
+    for w in range(4):
+        drained(rs_send[w].at[pl.ds(0, n - 1)], r.rs_s.at[w])
     for copy in local_copies:
         copy.wait()
-    for copy in sent:
-        copy.wait_send()
+
+
+def settle(*refs):
+    count = (len(refs) - 1) // 3
+    src, dst, mid, sems = refs[:count], refs[count : 2 * count], refs[2 * count : -1], refs[-1]
+    into = [pltpu.make_async_copy(src[i], mid[i], sems.at[0, i]) for i in range(count)]
+    out = [pltpu.make_async_copy(mid[i], dst[i], sems.at[1, i]) for i in range(count)]
+    for copy in into:
+        copy.start()
+    for i in range(count):
+        into[i].wait()
+        out[i].start()
+    for copy in out:
+        copy.wait()
 
 
 def whole_layer(n, m):
@@ -1270,7 +1291,16 @@
             lengths,
             pixel_mask,
         )
-        return result[:2] + (jnp.transpose(result[2], (1, 0, 2)),) + result[3:]
+        result = pl.pallas_call(
+            settle,
+            name="settle",
+            out_shape=[jax.ShapeDtypeStruct(a.shape, a.dtype) for a in result],
+            in_specs=[anywhere] * len(result),
+            out_specs=[anywhere] * len(result),
+            scratch_shapes=[pltpu.VMEM(a.shape, a.dtype) for a in result]
+            + [pltpu.SemaphoreType.DMA((2, len(result)))],
+        )(*result)
+        return (*result[:2], jnp.transpose(result[2], (1, 0, 2)), *result[3:])
 
     return on_each
 

time: 168 us -> 148 us (0.88)
  Pallas kernels: 158 us -> 147 us
  local copies, waits for them, and re-layouts: 8.59 us -> 0 us
    pallas_call x1, Pallas kernels: 158 us -> 144 us  [on_each(): pl.pallas_call(functools.partial(body, n, m, ins + outs + list(vm) + list...]
    unnamed x25 -> x0, local copies, waits for them, and re-layouts: 8.59 us -> none
    pallas_call x0 -> x1, Pallas kernels: none -> 2.7 us  [on_each(): pl.pallas_call(settle, name='settle', out_shape=[jax.ShapeDtypeStruct(a.s...]
where the time goes in v2:
time: 148 us
  Pallas kernels  147 us (99%)
    pallas_call x1, Pallas kernels, on_each(): pl.pallas_call(functools.partial(body, n, m, ins + outs + list(vm) + list...  144 us

profile of v2, /device:TPU:0, one launch (start us, length us, event | category | flops | bytes accessed | tf_op | source)
XLA Modules:
  0.0 147.9 jit_solution(9205715820832937791)
XLA Ops:
  0.6 144.3 %layer.1 = (f32[2,256,256]{2,1,0:T(8,128)}, f32[2,256,256]{2,1,0:T(8,128)}, f32[3,128,256]{2,1,0:T(8,128)}, f32[128,256]{1,0:T(8,128)}, f32[128,1024]{1,0:T(8,12...) custom-call(bf16[2,256,256]{2,1,0:T(8,128)(2,1)} %refs_0_.1, ...), custom_call_target="tpu_custom_call" | custom-call | tf_op jit(solution)/shard_map/layer/pallas_call | solution.py:1260
  145.0 2.7 %settle.1 = (f32[2,256,256]{2,1,0:T(8,128)}, f32[2,256,256]{2,1,0:T(8,128)}, f32[3,128,256]{2,1,0:T(8,128)}, f32[128,256]{1,0:T(8,128)}, f32[128,1024]{1,0:T(8,1...) custom-call(f32[2,256,256]{2,1,0:T(8,128)} %get-tuple-element.27.refs_0_, ...), custom_call_target="tpu_custom_call" | custom-call | tf_op jit(solution)/shard_map/settle/pallas_call | solution.py:1294

commit v3 on v2

--- a/solution.py
+++ b/solution.py
@@ -374,10 +374,10 @@
         "numer": ((tokens, local), F32),
         "denom": ((tokens, local), F32),
         "mixed": ((tokens, local), BF),
-        "st_send": ((batches, DH + 16, local), BF),
-        "st_recv": ((2, batches, DH + 16, local), BF),
-        "gs_send": ((batches, DH + 16, local), BF),
-        "gs_recv": ((2, batches, DH + 16, local), BF),
+        "st_send": ((batches * DH + 16, local), BF),
+        "st_recv": ((2, batches * DH + 16, local), BF),
+        "gs_send": ((batches * DH + 16, local), BF),
+        "gs_recv": ((2, batches * DH + 16, local), BF),
         "middle": ((own, width), F32),
         "ntwo": ((tokens, width), BF),
         "gelu_d": ((tokens, hidden), F32),
@@ -407,10 +407,6 @@
         "ru_r": ((n, block, hidden), BF),
         "rd_s": ((n, block, hidden), BF),
         "rd_r": ((n, block, hidden), BF),
-        "fq": ((3, block, local), F32),
-        "fo": ((block, local), F32),
-        "fu": ((block, hidden), F32),
-        "fd": ((block, hidden), F32),
         "hs_recv": ((m, 8, width), F32),
         "hs_send": ((8, width), F32),
         "upb": ((1, hidden), F32),
@@ -675,8 +671,7 @@
                 h,
             ).start()
 
-    finals = (r.fq, r.fo, r.fu, r.fd)
-    results = (r.gq_o, r.go_o, r.gu_o, r.gd_o)
+    finals = (r.gq_o, r.go_o, r.gu_o, r.gd_o)
     local_copies = []
 
     def rs_final(w):
@@ -690,10 +685,6 @@
                 for d in (0, 1):
                     v = v + rs_recv[w][(d * hops + hops - 1, *lead, slice(None), cols)].astype(F32)
                 finals[w][(*lead, slice(None), cols)] = v
-        copy = pltpu.make_async_copy(finals[w], results[w], r.lc.at[w])
-        copy.start()
-        local_copies.append(copy)
-
     def turn(k, src, dst):
         where = (hi, ds(lo * own, own))
         for i in range(1, m):
@@ -784,9 +775,9 @@
         ag_pass(OUT, j)
 
     crops(0)
-    for c in (0, 1):
-        hg_forward(0, c)
+    hg_forward(0, 0)
     ag_step(0)
+    hg_forward(0, 1)
     for copy in own_copies:
         copy.wait()
     r.smallg[:, ds(s * block, block)] = r.small[...]
@@ -847,18 +838,24 @@
 
     loop(tokens // tm, project)
 
-    def fold(matrix, total):
-        kept = jnp.where(same_head, matrix, 0.0)
-        acc = kept[0:DH]
-        for i in range(1, heads):
-            acc = acc + kept[i * DH : (i + 1) * DH]
-        top = lax.broadcasted_iota(jnp.int32, (16, local), 0) == 0
-        return acc.astype(BF), jnp.where(top, total, 0.0).astype(BF)
-
-    def unfold(ref):
-        acc = ref[0:DH, :].astype(F32)
-        wide = jnp.concatenate([acc] * heads, axis=0)
-        return jnp.where(same_head, wide, 0.0).astype(BF)
+    def fold(ref, parts):
+        row = lax.broadcasted_iota(jnp.int32, (16, local), 0)
+        sums = jnp.zeros((16, local), F32)
+        for b, (matrix, total) in enumerate(parts):
+            kept = jnp.where(same_head, matrix, 0.0)
+            acc = kept[0:DH]
+            for i in range(1, heads):
+                acc = acc + kept[i * DH : (i + 1) * DH]
+            ref[b * DH : (b + 1) * DH, :] = acc.astype(BF)
+            sums = jnp.where(row == b, total, sums)
+        ref[batches * DH :, :] = sums.astype(BF)
+
+    def unfold(ref, i, b):
+        acc = ref[i, b * DH : (b + 1) * DH, :].astype(F32)
+        return jnp.where(same_head, jnp.concatenate([acc] * heads, axis=0), 0.0).astype(BF)
+
+    def unfold_sum(ref, i, b):
+        return ref[i, batches * DH :, :].astype(F32)[b : b + 1]
 
     def state_send(k, ref, dest, step):
         for i in (0, 1):
@@ -877,12 +874,13 @@
             axis=0,
         )
 
+    parts = []
     for b in range(batches):
         k = r.kf[rows_of(b), :].astype(F32) * wide(r.tail[b])
-        moved = dot_tn(k.astype(BF), r.vf[rows_of(b), :])
-        a, t = fold(moved, jnp.sum(k, axis=0, keepdims=True))
-        r.st_send[b, 0:DH, :] = a
-        r.st_send[b, DH:, :] = t
+        parts.append(
+            (dot_tn(k.astype(BF), r.vf[rows_of(b), :]), jnp.sum(k, axis=0, keepdims=True))
+        )
+    fold(r.st_send, parts)
     state_send(0, r.st_send, r.st_recv, 1)
 
     for b in range(batches):
@@ -907,12 +905,18 @@
 
     for b in range(batches):
         left = both(b, r.qf[rows_of(b), :], before_thr[b])
-        states = jnp.concatenate([unfold(r.st_recv.at[i, b]) for i in (0, 1)], axis=0)
+        states = jnp.concatenate([unfold(r.st_recv, i, b) for i in (0, 1)], axis=0)
+        only = lax.broadcasted_iota(jnp.int32, (16, local), 0)
         sums = jnp.concatenate(
             [
                 jnp.where(
                     same_head,
-                    dot_tn(r.st_recv[i, b, DH:, :], jnp.ones((16, local), BF)),
+                    dot_tn(
+                        jnp.where(
+                            only == b, r.st_recv[i, batches * DH :, :].astype(F32), 0.0
+                        ).astype(BF),
+                        jnp.ones((16, local), BF),
+                    ),
                     0.0,
                 ).astype(BF)
                 for i in (0, 1)
@@ -979,6 +983,7 @@
     loop((tokens // tu) * (hidden // tn), up)
     rs_round(DOWN, 0)
     ag_pass(DOWN, 2)
+    rs_round(DOWN, 1)
     ag_wait(DOWN, 3)
 
     def back(i):
@@ -991,10 +996,9 @@
     rs_round(UP, 0)
     hr_first(2, 0, pick(r.g_hid), product_nt(r.wu))
     hr_first(2, 1, pick(r.g_hid), product_nt(r.wu))
-    rs_round(DOWN, 1)
     hr_second(2, 0)
     hr_second(2, 1)
-    rs_round(UP, 1)
+    rs_round(DOWN, 2)
 
     r.hs_send[...] = jnp.zeros_like(r.hs_send)
 
@@ -1019,13 +1023,20 @@
 
         loop(part_rows // tile, some)
 
-    for c in (0, 1):
-        hr_wait(2, c)
-        norm_two_back(c)
-        hg_start(3, c)
-    rs_round(DOWN, 2)
+    hr_wait(2, 0)
+    norm_two_back(0)
+    hg_start(3, 0)
+    rs_round(UP, 1)
+    hr_wait(2, 1)
+    norm_two_back(1)
+    hg_start(3, 1)
+    hr_first(1, 0, pick(r.activ), product_nt(r.wd))
+    hr_first(1, 1, pick(r.activ), product_nt(r.wd))
+    rs_round(DOWN, 3)
     for c in (0, 1):
         hg_forward(3, c)
+    for c in (0, 1):
+        hr_second(1, c)
     for c in (0, 1):
         hg_finish(3, c)
 
@@ -1047,12 +1058,16 @@
 
     loop(tokens // tm, mixed_back)
 
+    parts = []
     for b in range(batches):
         q = r.qf[rows_of(b), :].astype(F32) * wide(r.car[b])
-        moved = dot_tn(q.astype(BF), r.g_num[rows_of(b), :])
-        a, t = fold(moved, jnp.sum(q * r.g_den[rows_of(b), :], axis=0, keepdims=True))
-        r.gs_send[b, 0:DH, :] = a
-        r.gs_send[b, DH:, :] = t
+        parts.append(
+            (
+                dot_tn(q.astype(BF), r.g_num[rows_of(b), :]),
+                jnp.sum(q * r.g_den[rows_of(b), :], axis=0, keepdims=True),
+            )
+        )
+    fold(r.gs_send, parts)
     state_send(1, r.gs_send, r.gs_recv, -1)
     rs_round(UP, 2)
 
@@ -1072,11 +1087,8 @@
             gk = gk + dot_tn(g, head_lanes(hd, r.qf[rw, :]))
             gv = gv + dot_tn(r.low[b, :, hd * rows : (hd + 1) * rows], gn)
         left = both(b, r.g_num[rw, :], before_thr[b])
-        states = jnp.concatenate([unfold(r.st_recv.at[i, b]) for i in (0, 1)], axis=1)
-        totals = (
-            r.st_recv[0, b, DH : DH + 16, :].astype(F32)[0:1]
-            + before_thr[b] * r.st_recv[1, b, DH : DH + 16, :].astype(F32)[0:1]
-        )
+        states = jnp.concatenate([unfold(r.st_recv, i, b) for i in (0, 1)], axis=1)
+        totals = unfold_sum(r.st_recv, 0, b) + before_thr[b] * unfold_sum(r.st_recv, 1, b)
         gq = gq + dot_nt(left, states) + wide(r.car[b]) * r.g_den[rw, :] * totals
         r.gproj[0, rw, :] = (gq * r.phi_d[0, rw, :]).astype(BF)
         r.gk[rw, :] = gk
@@ -1087,11 +1099,8 @@
     for b in range(batches):
         rw = rows_of(b)
         thr = after_thr[b]
-        states = [unfold(r.gs_recv.at[i, b]) for i in (0, 1)]
-        totals = (
-            r.gs_recv[0, b, DH : DH + 16, :].astype(F32)[0:1]
-            + thr * r.gs_recv[1, b, DH : DH + 16, :].astype(F32)[0:1]
-        )
+        states = [unfold(r.gs_recv, i, b) for i in (0, 1)]
+        totals = unfold_sum(r.gs_recv, 0, b) + thr * unfold_sum(r.gs_recv, 1, b)
         k = r.kf[rw, :].astype(F32) * wide(r.tail[b])
         v = r.vf[rw, :].astype(F32) * wide(r.tail[b])
         k2 = jnp.concatenate([k.astype(BF), (k * thr).astype(BF)], axis=1)
@@ -1102,7 +1111,6 @@
         r.gproj[2, rw, :] = gv.astype(BF)
 
     rs_round(QKV, 0)
-    rs_round(DOWN, 3)
 
     def picks(where):
         return [
@@ -1119,13 +1127,9 @@
     hr_first(3, 1, picks, first_term)
     hr_second(3, 0)
     hr_second(3, 1)
+    rs_round(OUT, 1)
     rs_round(QKV, 1)
-    rs_round(OUT, 1)
     rs_round(UP, 3)
-    hr_first(1, 0, pick(r.activ), product_nt(r.wd))
-    hr_first(1, 1, pick(r.activ), product_nt(r.wd))
-    hr_second(1, 0)
-    hr_second(1, 1)
 
     def norm_one_back(c):
         def some(i):
@@ -1171,6 +1175,7 @@
     loop(tokens // tile, column_sums)
     rs_round(OUT, 3)
     rs_final(DOWN)
+    rs_round(QKV, 3)
     landed(r.hs_recv.at[pl.ds(0, m - 1)], r.hs_r.at[0])
     acc = r.hs_recv[0]
     for i in range(1, m):
@@ -1189,7 +1194,6 @@
             h,
         ).start()
     rs_final(UP)
-    rs_round(QKV, 3)
     rs_final(OUT)
     landed(r.ss_recv.at[pl.ds(0, n - 1)], r.ss_r.at[0])
     acc = r.ss_recv[0]
@@ -1226,16 +1230,13 @@
 
 
 def settle(*refs):
-    count = (len(refs) - 1) // 3
-    src, dst, mid, sems = refs[:count], refs[count : 2 * count], refs[2 * count : -1], refs[-1]
-    into = [pltpu.make_async_copy(src[i], mid[i], sems.at[0, i]) for i in range(count)]
-    out = [pltpu.make_async_copy(mid[i], dst[i], sems.at[1, i]) for i in range(count)]
-    for copy in into:
+    count = len(refs) // 2
+    copies = [
+        pltpu.make_async_copy(refs[i], refs[count + i], refs[-1].at[i]) for i in range(count)
+    ]
+    for copy in copies:
         copy.start()
-    for i in range(count):
-        into[i].wait()
-        out[i].start()
-    for copy in out:
+    for copy in copies:
         copy.wait()
 
 
@@ -1254,29 +1255,26 @@
         in_vmem = pl.BlockSpec(memory_space=pltpu.VMEM)
         in_smem = pl.BlockSpec(memory_space=pltpu.SMEM)
 
-        def wide(*shape):
-            return jax.ShapeDtypeStruct(shape, F32)
-
         result = pl.pallas_call(
             functools.partial(body, n, m, ins + outs + list(vm) + list(sems)),
             name="layer",
             out_shape=(
-                wide(batches, rows, local),
-                wide(batches, rows, local),
-                wide(3, block, local),
-                wide(block, local),
-                wide(block, hidden),
-                wide(block, hidden),
-                wide(2, block),
-                wide(3, block),
-                wide(1, block),
+                pltpu.VMEM((batches, rows, local), F32),
+                pltpu.VMEM((batches, rows, local), F32),
+                pltpu.VMEM((3, block, local), F32),
+                pltpu.VMEM((block, local), F32),
+                pltpu.VMEM((block, hidden), F32),
+                pltpu.VMEM((block, hidden), F32),
+                pltpu.VMEM((2, block), F32),
+                pltpu.VMEM((3, block), F32),
+                pltpu.VMEM((1, block), F32),
             ),
             in_specs=[anywhere] * 6 + [in_vmem] * 3 + [in_smem, in_vmem],
-            out_specs=[anywhere] * 6 + [in_vmem] * 3,
+            out_specs=[in_vmem] * 9,
             scratch_shapes=[pltpu.VMEM(shape, kind) for shape, kind in vm.values()]
             + [pltpu.SemaphoreType.DMA(shape) for shape in sems.values()],
             compiler_params=pltpu.CompilerParams(
-                collective_id=0, has_side_effects=True, vmem_limit_bytes=66_000_000
+                collective_id=0, has_side_effects=True, vmem_limit_bytes=60_000_000
             ),
         )(
             tokens,
@@ -1295,11 +1293,10 @@
             settle,
             name="settle",
             out_shape=[jax.ShapeDtypeStruct(a.shape, a.dtype) for a in result],
-            in_specs=[anywhere] * len(result),
+            in_specs=[in_vmem] * len(result),
             out_specs=[anywhere] * len(result),
-            scratch_shapes=[pltpu.VMEM(a.shape, a.dtype) for a in result]
-            + [pltpu.SemaphoreType.DMA((2, len(result)))],
-        )(*result)
+            scratch_shapes=[pltpu.SemaphoreType.DMA((len(result),))],
+        )(*[pltpu.with_memory_space_constraint(a, pltpu.VMEM) for a in result])
         return (*result[:2], jnp.transpose(result[2], (1, 0, 2)), *result[3:])
 
     return on_each

time: 148 us -> 141 us (0.953)
  Pallas kernels: 147 us -> 140 us
    pallas_call x1, Pallas kernels: 144 us -> 139 us  [on_each(): pl.pallas_call(functools.partial(body, n, m, ins + outs + list(vm) + list...]
where the time goes in v3:
time: 141 us
  Pallas kernels  140 us (99%)
    pallas_call x1, Pallas kernels, on_each(): pl.pallas_call(functools.partial(body, n, m, ins + outs + list(vm) + list...  139 us

profile of v3, /device:TPU:0, one launch (start us, length us, event | category | flops | bytes accessed | tf_op | source)
XLA Modules:
  0.0 140.9 jit_solution(11325561907387176180)
XLA Ops:
  0.6 138.5 %layer.1 = (f32[2,256,256]{2,1,0:T(8,128)S(1)}, f32[2,256,256]{2,1,0:T(8,128)S(1)}, f32[3,128,256]{2,1,0:T(8,128)S(1)}, f32[128,256]{1,0:T(8,128)S(1)}, f32[128,...) custom-call(bf16[2,256,256]{2,1,0:T(8,128)(2,1)} %refs_0_.1, ...), custom_call_target="tpu_custom_call" | custom-call | tf_op jit(solution)/shard_map/layer/pallas_call | solution.py:1258
  139.2 1.6 %settle.1 = (f32[2,256,256]{2,1,0:T(8,128)}, f32[2,256,256]{2,1,0:T(8,128)}, f32[3,128,256]{2,1,0:T(8,128)}, f32[128,256]{1,0:T(8,128)}, f32[128,1024]{1,0:T(8,1...) custom-call(f32[2,256,256]{2,1,0:T(8,128)S(1)} %get-tuple-element.27.refs_0_, ...), custom_call_target="tpu_custom_call" | custom-call | tf_op jit(solution)/shard_map/settle/pallas_call | solution.py:1292

commit v4 on v3

--- a/solution.py
+++ b/solution.py
@@ -432,7 +432,7 @@
         "hs_r": (1,),
         "ss_s": (1,),
         "ss_r": (1,),
-        "lc": (12,),
+        "lc": (8,),
     }
     return vm, sems
 
@@ -650,14 +650,14 @@
     def rs_round(w, step):
         for d in (0, 1):
             slot = d * hops + step
+            owner = at(p + sign[d] * (hops - step))
+            pieces = (0, 1) if step > 0 else (d,)
+            terms = [rs_term(w, owner, piece) for piece in pieces]
             if step > 0:
                 rs_arrived(w, d, step - 1)
-            for piece in (0, 1):
-                if step == 0 and piece != d:
-                    continue
-                terms = rs_term(w, at(p + sign[d] * (hops - step)), piece)
+            for piece, parts in zip(pieces, terms):
                 cols = rs_half(w, piece)
-                for i, v in enumerate(terms):
+                for i, v in enumerate(parts):
                     lead = (i,) if w == QKV else ()
                     if step > 1 or (step == 1 and piece == d):
                         v = v + rs_recv[w][(slot - 1, *lead, slice(None), cols)].astype(F32)
@@ -698,7 +698,7 @@
                 to,
             ).start()
         copy = pltpu.make_async_copy(
-            src.at[:, ds(h * local, local)], dst.at[where[0], where[1], :], r.lc.at[4 + k]
+            src.at[:, ds(h * local, local)], dst.at[where[0], where[1], :], r.lc.at[k]
         )
         copy.start()
         local_copies.append(copy)
@@ -712,12 +712,12 @@
     hg_start(0, 0)
     hg_start(0, 1)
     own_copies = [
-        pltpu.make_async_copy(r.w_qkv, r.wq.at[:, ds(s * block, block), :], r.lc.at[8]),
-        pltpu.make_async_copy(r.w_out, r.wo.at[ds(s * block, block), :], r.lc.at[9]),
-        pltpu.make_async_copy(r.w_up, r.wu.at[ds(s * block, block), :], r.lc.at[10]),
-        pltpu.make_async_copy(r.w_down, r.wd.at[ds(s * block, block), :], r.lc.at[11]),
-        pltpu.make_async_copy(r.tok, r.xg.at[:, :, ds(h * local, local)], r.lc.at[6]),
-        pltpu.make_async_copy(r.cot, r.cg.at[:, :, ds(h * local, local)], r.lc.at[7]),
+        pltpu.make_async_copy(r.w_qkv, r.wq.at[:, ds(s * block, block), :], r.lc.at[4]),
+        pltpu.make_async_copy(r.w_out, r.wo.at[ds(s * block, block), :], r.lc.at[5]),
+        pltpu.make_async_copy(r.w_up, r.wu.at[ds(s * block, block), :], r.lc.at[6]),
+        pltpu.make_async_copy(r.w_down, r.wd.at[ds(s * block, block), :], r.lc.at[7]),
+        pltpu.make_async_copy(r.tok, r.xg.at[:, :, ds(h * local, local)], r.lc.at[2]),
+        pltpu.make_async_copy(r.cot, r.cg.at[:, :, ds(h * local, local)], r.lc.at[3]),
     ]
     for copy in own_copies:
         copy.start()
@@ -997,8 +997,8 @@
     hr_first(2, 0, pick(r.g_hid), product_nt(r.wu))
     hr_first(2, 1, pick(r.g_hid), product_nt(r.wu))
     hr_second(2, 0)
+    rs_round(DOWN, 2)
     hr_second(2, 1)
-    rs_round(DOWN, 2)
 
     r.hs_send[...] = jnp.zeros_like(r.hs_send)
 

time: 141 us -> 140 us (level)
  no operation moved by 1% of the time
where the time goes in v4:
time: 140 us
  Pallas kernels  139 us (99%)
    pallas_call x1, Pallas kernels, on_each(): pl.pallas_call(functools.partial(body, n, m, ins + outs + list(vm) + list...  138 us

profile of v4, /device:TPU:0, one launch (start us, length us, event | category | flops | bytes accessed | tf_op | source)
XLA Modules:
  0.0 140.0 jit_solution(18104526119069274313)
XLA Ops:
  0.6 137.6 %layer.1 = (f32[2,256,256]{2,1,0:T(8,128)S(1)}, f32[2,256,256]{2,1,0:T(8,128)S(1)}, f32[3,128,256]{2,1,0:T(8,128)S(1)}, f32[128,256]{1,0:T(8,128)S(1)}, f32[128,...) custom-call(bf16[2,256,256]{2,1,0:T(8,128)(2,1)} %refs_0_.1, ...), custom_call_target="tpu_custom_call" | custom-call | tf_op jit(solution)/shard_map/layer/pallas_call | solution.py:1258
  138.3 1.6 %settle.1 = (f32[2,256,256]{2,1,0:T(8,128)}, f32[2,256,256]{2,1,0:T(8,128)}, f32[3,128,256]{2,1,0:T(8,128)}, f32[128,256]{1,0:T(8,128)}, f32[128,1024]{1,0:T(8,1...) custom-call(f32[2,256,256]{2,1,0:T(8,128)S(1)} %get-tuple-element.27.refs_0_, ...), custom_call_target="tpu_custom_call" | custom-call | tf_op jit(solution)/shard_map/settle/pallas_call | solution.py:1292

commit v5 on v4

--- a/solution.py
+++ b/solution.py
@@ -320,6 +320,7 @@
 BF = jnp.bfloat16
 F32 = jnp.float32
 QKV, OUT, UP, DOWN, SMALL = range(5)
+QUERY = 4
 
 
 def dot_nn(a, b):
@@ -399,14 +400,22 @@
         "h_acc": ((4, 2, 2, own // 2, width), F32),
         "h_s2": ((4, 2, own // 2, width), BF),
         "h_r2": ((4, 2, own // 2, width), BF),
-        "rq_s": ((n, 3, block, local), BF),
-        "rq_r": ((n, 3, block, local), BF),
+        "rq_s": ((n, 2, block, local), BF),
+        "rq_r": ((n, 2, block, local), BF),
+        "rx_s": ((n, block, local), BF),
+        "rx_r": ((n, block, local), BF),
         "ro_s": ((n, block, local), BF),
         "ro_r": ((n, block, local), BF),
         "ru_s": ((n, block, hidden), BF),
         "ru_r": ((n, block, hidden), BF),
         "rd_s": ((n, block, hidden), BF),
         "rd_r": ((n, block, hidden), BF),
+        "pq": ((2, 2, block, local), F32),
+        "po": ((2, block, local), F32),
+        "pu": ((2, block, hidden), F32),
+        "pd": ((2, block, hidden), F32),
+        "px": ((2, block, local), F32),
+        "g_act": ((tokens, hidden), F32),
         "hs_recv": ((m, 8, width), F32),
         "hs_send": ((8, width), F32),
         "upb": ((1, hidden), F32),
@@ -418,8 +427,8 @@
     sems = {
         "ag_s": (5,),
         "ag_r": (5, 2, hops),
-        "rs_s": (4,),
-        "rs_r": (4, 2, hops),
+        "rs_s": (5,),
+        "rs_r": (5, 2, hops),
         "hg_s": (4,),
         "hg_r": (4, 2, 3),
         "hr_s": (4, 2),
@@ -628,10 +637,11 @@
         if w == OUT:
             return [dot_tn(r.gatt[:, cols], r.mixed[:, pl.ds(piece * half, half)])]
         left = r.normed[:, cols]
-        return [dot_tn(left, r.gproj[i, :, pl.ds(piece * half, half)]) for i in range(3)]
-
-    rs_send = (r.rq_s, r.ro_s, r.ru_s, r.rd_s)
-    rs_recv = (r.rq_r, r.ro_r, r.ru_r, r.rd_r)
+        kinds = (0,) if w == QUERY else (1, 2)
+        return [dot_tn(left, r.gproj[i, :, pl.ds(piece * half, half)]) for i in kinds]
+
+    rs_send = (r.rq_s, r.ro_s, r.ru_s, r.rd_s, r.rx_s)
+    rs_recv = (r.rq_r, r.ro_r, r.ru_r, r.rd_r, r.rx_r)
 
     def rs_half(w, piece):
         half = rs_send[w].shape[-1] // 2
@@ -647,18 +657,29 @@
     def rs_arrived(w, d, step):
         landed(rs_view(rs_recv[w], w, d, step), r.rs_r.at[w, d, step])
 
+    ahead = (r.pq, r.po, r.pu, r.pd, r.px)
+
+    def rs_prepare(w, step):
+        for d in (0, 1) if step < hops else (0,):
+            owner = at(p + sign[d] * (hops - step)) if step < hops else s
+            for piece in (0, 1) if step > 0 else (d,):
+                cols = rs_half(w, piece)
+                for i, v in enumerate(rs_term(w, owner, piece)):
+                    lead = (i,) if w == QKV else ()
+                    ahead[w][(d, *lead, slice(None), cols)] = v
+
     def rs_round(w, step):
+        if step == 0:
+            rs_prepare(w, 0)
         for d in (0, 1):
             slot = d * hops + step
-            owner = at(p + sign[d] * (hops - step))
-            pieces = (0, 1) if step > 0 else (d,)
-            terms = [rs_term(w, owner, piece) for piece in pieces]
             if step > 0:
                 rs_arrived(w, d, step - 1)
-            for piece, parts in zip(pieces, terms):
+            for piece in (0, 1) if step > 0 else (d,):
                 cols = rs_half(w, piece)
-                for i, v in enumerate(parts):
+                for i in range(2 if w == QKV else 1):
                     lead = (i,) if w == QKV else ()
+                    v = ahead[w][(d, *lead, slice(None), cols)]
                     if step > 1 or (step == 1 and piece == d):
                         v = v + rs_recv[w][(slot - 1, *lead, slice(None), cols)].astype(F32)
                     rs_send[w][(slot, *lead, slice(None), cols)] = v.astype(BF)
@@ -670,21 +691,23 @@
                 ring[d],
                 h,
             ).start()
-
-    finals = (r.gq_o, r.go_o, r.gu_o, r.gd_o)
+        rs_prepare(w, step + 1)
+
+    finals = (r.gq_o.at[pl.ds(1, 2)], r.go_o, r.gu_o, r.gd_o, r.gq_o.at[0])
     local_copies = []
 
     def rs_final(w):
-        terms = [rs_term(w, s, piece) for piece in (0, 1)]
         for d in (0, 1):
             rs_arrived(w, d, hops - 1)
         for piece in (0, 1):
             cols = rs_half(w, piece)
-            for i, v in enumerate(terms[piece]):
+            for i in range(2 if w == QKV else 1):
                 lead = (i,) if w == QKV else ()
+                v = ahead[w][(0, *lead, slice(None), cols)]
                 for d in (0, 1):
                     v = v + rs_recv[w][(d * hops + hops - 1, *lead, slice(None), cols)].astype(F32)
                 finals[w][(*lead, slice(None), cols)] = v
+
     def turn(k, src, dst):
         where = (hi, ds(lo * own, own))
         for i in range(1, m):
@@ -981,23 +1004,36 @@
         )
 
     loop((tokens // tu) * (hidden // tn), up)
+    near = [ds(at(p + n + i) * block, block) for i in range(1 - hops, hops)]
+
+    def back_near(i):
+        cols = ds(i * tn, tn)
+        right = jnp.concatenate([r.wd[rw, cols] for rw in near], axis=0)
+        for b in range(batches):
+            left = jnp.concatenate([r.cg[b, :, rw] for rw in near], axis=1)
+            r.g_act[rows_of(b), cols] = dot_nn(left, right)
+
     rs_round(DOWN, 0)
     ag_pass(DOWN, 2)
     rs_round(DOWN, 1)
+    loop(hidden // tn, back_near)
     ag_wait(DOWN, 3)
+
+    far_block = ds(at(p + hops) * block, block)
 
     def back(i):
         cols = ds(i * tn, tn)
         for b in range(batches):
-            g = dot_nn(r.cg[b], r.wd[:, cols])
-            r.g_hid[rows_of(b), cols] = (g * r.gelu_d[rows_of(b), cols]).astype(BF)
+            rw = rows_of(b)
+            g = r.g_act[rw, cols] + dot_nn(r.cg[b, :, far_block], r.wd[far_block, cols])
+            r.g_hid[rw, cols] = (g * r.gelu_d[rw, cols]).astype(BF)
 
     loop(hidden // tn, back)
     rs_round(UP, 0)
     hr_first(2, 0, pick(r.g_hid), product_nt(r.wu))
     hr_first(2, 1, pick(r.g_hid), product_nt(r.wu))
+    rs_round(DOWN, 2)
     hr_second(2, 0)
-    rs_round(DOWN, 2)
     hr_second(2, 1)
 
     r.hs_send[...] = jnp.zeros_like(r.hs_send)
@@ -1095,6 +1131,7 @@
         r.gv[rw, :] = gv
 
     rs_round(OUT, 0)
+    rs_round(QUERY, 0)
     state_wait(1, r.gs_recv)
     for b in range(batches):
         rw = rows_of(b)
@@ -1128,6 +1165,7 @@
     hr_second(3, 0)
     hr_second(3, 1)
     rs_round(OUT, 1)
+    rs_round(QUERY, 1)
     rs_round(QKV, 1)
     rs_round(UP, 3)
 
@@ -1148,6 +1186,7 @@
         norm_one_back(c)
     turn(1, r.i_rows, r.ing_o)
     rs_round(OUT, 2)
+    rs_round(QUERY, 2)
     rs_round(QKV, 2)
 
     def finish_rows(c):
@@ -1174,6 +1213,7 @@
 
     loop(tokens // tile, column_sums)
     rs_round(OUT, 3)
+    rs_round(QUERY, 3)
     rs_final(DOWN)
     rs_round(QKV, 3)
     landed(r.hs_recv.at[pl.ds(0, m - 1)], r.hs_r.at[0])
@@ -1195,6 +1235,7 @@
         ).start()
     rs_final(UP)
     rs_final(OUT)
+    rs_final(QUERY)
     landed(r.ss_recv.at[pl.ds(0, n - 1)], r.ss_r.at[0])
     acc = r.ss_recv[0]
     for i in range(1, n):
@@ -1223,7 +1264,7 @@
     drained(r.hs_recv.at[pl.ds(0, m - 1)], r.hs_s.at[0])
     drained(r.ss_recv.at[pl.ds(0, n - 1)], r.ss_s.at[0])
     rs_final(QKV)
-    for w in range(4):
+    for w in range(5):
         drained(rs_send[w].at[pl.ds(0, n - 1)], r.rs_s.at[w])
     for copy in local_copies:
         copy.wait()

time: 140 us -> 137 us (0.979)
  Pallas kernels: 139 us -> 136 us
    pallas_call x1, Pallas kernels: 138 us -> 134 us  [on_each(): pl.pallas_call(functools.partial(body, n, m, ins + outs + list(vm) + list...]
where the time goes in v5:
time: 137 us
  Pallas kernels  136 us (99%)
    pallas_call x1, Pallas kernels, on_each(): pl.pallas_call(functools.partial(body, n, m, ins + outs + list(vm) + list...  134 us

profile of v5, /device:TPU:0, one launch (start us, length us, event | category | flops | bytes accessed | tf_op | source)
XLA Modules:
  0.0 136.6 jit_solution(5550800216786153104)
XLA Ops:
  0.6 134.2 %layer.1 = (f32[2,256,256]{2,1,0:T(8,128)S(1)}, f32[2,256,256]{2,1,0:T(8,128)S(1)}, f32[3,128,256]{2,1,0:T(8,128)S(1)}, f32[128,256]{1,0:T(8,128)S(1)}, f32[128,...) custom-call(bf16[2,256,256]{2,1,0:T(8,128)(2,1)} %refs_0_.1, ...), custom_call_target="tpu_custom_call" | custom-call | tf_op jit(solution)/shard_map/layer/pallas_call | solution.py:1299
  134.9 1.6 %settle.1 = (f32[2,256,256]{2,1,0:T(8,128)}, f32[2,256,256]{2,1,0:T(8,128)}, f32[3,128,256]{2,1,0:T(8,128)}, f32[128,256]{1,0:T(8,128)}, f32[128,1024]{1,0:T(8,1...) custom-call(f32[2,256,256]{2,1,0:T(8,128)S(1)} %get-tuple-element.27.refs_0_, ...), custom_call_target="tpu_custom_call" | custom-call | tf_op jit(solution)/shard_map/settle/pallas_call | solution.py:1333

commit v6 on v5

--- a/solution.py
+++ b/solution.py
@@ -428,11 +428,10 @@
         "ag_s": (5,),
         "ag_r": (5, 2, hops),
         "rs_s": (5,),
-        "rs_r": (5, 2, hops),
         "hg_s": (4,),
-        "hg_r": (4, 2, 3),
+        "hg_r": (2, 2, 3),
         "hr_s": (4, 2),
-        "hr_r": (4, 2, 2),
+        "hr_r": (2, 2, 2),
         "st_s": (2,),
         "st_r": (2,),
         "aa_s": (2,),
@@ -554,7 +553,7 @@
         return (r.ntwo, r.gatt)[k - 2].at[ds(who * own + c * part_rows, part_rows), :]
 
     def hg_copy(k, c, i, src, who, to):
-        return remote(src, hg_view(k, c, who), r.hg_s.at[k], r.hg_r.at[k, c, i], s, to)
+        return remote(src, hg_view(k, c, who), r.hg_s.at[k], r.hg_r.at[k % 2, c, i], s, to)
 
     def hg_start(k, c):
         src = (r.tok, r.cot)[k].at[c] if k < 2 else hg_view(k, c, h)
@@ -594,7 +593,7 @@
             src, dst, to = r.h_s1.at[k, c], r.h_r1.at[k, c], pair
         else:
             src, dst, to = r.h_s2.at[k, c], r.h_r2.at[k, c], cross
-        return remote(src, dst, r.hr_s.at[k, stage], r.hr_r.at[k, c, stage], s, to)
+        return remote(src, dst, r.hr_s.at[k, stage], r.hr_r.at[k // 2, c, stage], s, to)
 
     def hr_second(k, c):
         hr_copy(k, c, 0).wait_recv()
@@ -655,7 +654,7 @@
         return ref.at[d * hops, :, rs_half(w, d)]
 
     def rs_arrived(w, d, step):
-        landed(rs_view(rs_recv[w], w, d, step), r.rs_r.at[w, d, step])
+        landed(rs_view(rs_recv[w], w, d, step), r.ag_r.at[w, d, step])
 
     ahead = (r.pq, r.po, r.pu, r.pd, r.px)
 
@@ -687,7 +686,7 @@
                 rs_view(rs_send[w], w, d, step),
                 rs_view(rs_recv[w], w, d, step),
                 r.rs_s.at[w],
-                r.rs_r.at[w, d, step],
+                r.ag_r.at[w, d, step],
                 ring[d],
                 h,
             ).start()
@@ -848,16 +847,19 @@
         b = lax.div(i, rows // tm)
         rb = ds(lax.rem(i, rows // tm) * tm, tm)
         left = r.normed[rw, :]
-        for kind in (0, 1):
-            v = dot_nn(left, r.wq[kind])
-            low = jnp.exp(jnp.minimum(v, 0.0))
-            f = jnp.where(v > 0.0, v + 1.0, low).astype(BF)
-            r.phi_d[kind, rw, :] = low
-            if kind == 0:
-                r.qf[rw, :] = f
-            else:
-                r.kf[rw, :] = (f.astype(F32) * wide(r.pmc[b, rb, :])).astype(BF)
+        v = dot_nn(left, r.wq[1])
+        low = jnp.exp(jnp.minimum(v, 0.0))
+        f = jnp.where(v > 0.0, v + 1.0, low).astype(BF)
+        r.phi_d[1, rw, :] = low
+        r.kf[rw, :] = (f.astype(F32) * wide(r.pmc[b, rb, :])).astype(BF)
         r.vf[rw, :] = dot_nn(left, r.wq[2]).astype(BF)
+
+    def project_query(i):
+        rw = ds(i * tm, tm)
+        v = dot_nn(r.normed[rw, :], r.wq[0])
+        low = jnp.exp(jnp.minimum(v, 0.0))
+        r.phi_d[0, rw, :] = low
+        r.qf[rw, :] = jnp.where(v > 0.0, v + 1.0, low).astype(BF)
 
     loop(tokens // tm, project)
 
@@ -905,6 +907,7 @@
         )
     fold(r.st_send, parts)
     state_send(0, r.st_send, r.st_recv, 1)
+    loop(tokens // tm, project_query)
 
     for b in range(batches):
         q, k = r.qf[rows_of(b), :], r.kf[rows_of(b), :]

time: 137 us -> 136 us (level)
  no operation moved by 1% of the time
where the time goes in v6:
time: 136 us
  Pallas kernels  135 us (99%)
    pallas_call x1, Pallas kernels, on_each(): pl.pallas_call(functools.partial(body, n, m, ins + outs + list(vm) + list...  133 us

profile of v6, /device:TPU:0, one launch (start us, length us, event | category | flops | bytes accessed | tf_op | source)
XLA Modules:
  0.0 135.7 jit_solution(8821321759814875532)
XLA Ops:
  0.6 133.3 %layer.1 = (f32[2,256,256]{2,1,0:T(8,128)S(1)}, f32[2,256,256]{2,1,0:T(8,128)S(1)}, f32[3,128,256]{2,1,0:T(8,128)S(1)}, f32[128,256]{1,0:T(8,128)S(1)}, f32[128,...) custom-call(bf16[2,256,256]{2,1,0:T(8,128)(2,1)} %refs_0_.1, ...), custom_call_target="tpu_custom_call" | custom-call | tf_op jit(solution)/shard_map/layer/pallas_call | solution.py:1302
  134.0 1.6 %settle.1 = (f32[2,256,256]{2,1,0:T(8,128)}, f32[2,256,256]{2,1,0:T(8,128)}, f32[3,128,256]{2,1,0:T(8,128)}, f32[128,256]{1,0:T(8,128)}, f32[128,1024]{1,0:T(8,1...) custom-call(f32[2,256,256]{2,1,0:T(8,128)S(1)} %get-tuple-element.27.refs_0_, ...), custom_call_target="tpu_custom_call" | custom-call | tf_op jit(solution)/shard_map/settle/pallas_call | solution.py:1336

commit v7 on v6

--- a/solution.py
+++ b/solution.py
@@ -493,14 +493,61 @@
     def landed(view, sem):
         remote(view, view, sem, sem, ring[0], h).wait_recv()
 
+    barrier = pltpu.get_barrier_semaphore()
+    for peer in ((ring[0], h), (ring[1], h), (s, pair), (s, cross)):
+        pl.semaphore_signal(barrier, inc=1, device_id=peer, device_id_type=MESH)
+
     r.small[...] = jnp.zeros_like(r.small)
     r.small[0:2, :] = r.gains[...].astype(F32)
     r.small[2:5, :] = r.biases[...].astype(F32)
     r.small[5:6, :] = r.up_bias[...].astype(F32)
 
-    barrier = pltpu.get_barrier_semaphore()
-    for peer in ((ring[0], h), (ring[1], h), (s, pair), (s, cross)):
-        pl.semaphore_signal(barrier, inc=1, device_id=peer, device_id_type=MESH)
+    first = s * rows
+    row_at = lax.broadcasted_iota(jnp.int32, (rows, 128), 0)
+    lane_at = lax.broadcasted_iota(jnp.int32, (rows, rows), 1)
+    square = lax.broadcasted_iota(jnp.int32, (local, local), 0)
+    square_lane = lax.broadcasted_iota(jnp.int32, (local, local), 1)
+    same_head = (square // DH) == (square_lane // DH)
+    diagonal = square == square_lane
+    lane_head = lax.broadcasted_iota(jnp.int32, (rows, local), 1) // DH
+    before_thr, after_thr = [], []
+
+    def wide(value):
+        return jnp.concatenate([value] * (local // 128), axis=1)
+
+    def begin(offsets, place):
+        value = 0
+        for off in offsets:
+            value = jnp.where(off <= place, off, value)
+        return value
+
+    def through(offsets, which):
+        return jnp.where(
+            begin(offsets, which * rows + rows - 1) < which * rows, 1.0, 0.0
+        ).astype(F32)
+
+    def crops(b):
+        offsets, running = [], 0
+        for i in range(r.lengths.shape[1]):
+            offsets.append(running)
+            running = running + r.lengths[b, i]
+        start = jnp.zeros((rows, 128), jnp.int32)
+        for off in offsets:
+            start = jnp.where(off <= row_at + first, off, start)
+        last = begin(offsets, first + rows - 1)
+        r.mask[b] = jnp.where(
+            (lane_at + first >= wide(start)) & (lane_at <= wide(row_at)), 1.0, 0.0
+        ).astype(F32)
+        r.car[b] = jnp.where(start < first, 1.0, 0.0).astype(F32)
+        r.tail[b] = jnp.where(start == last, 1.0, 0.0).astype(F32)
+        before_thr.append(through(offsets, lax.rem(s + n - 1, n)))
+        after_thr.append(through(offsets, lax.rem(s + 1, n)))
+        keep = r.pixel[b : b + 1, :].astype(F32)
+        r.pmc[b] = dot_nn(
+            jnp.where(diagonal, keep, 0.0).astype(BF), jnp.ones((rows, 128), BF)
+        )
+
+    crops(0)
     pl.semaphore_wait(barrier, 4)
 
     shards = (r.w_qkv, r.w_out, r.w_up, r.w_down, r.small)
@@ -746,57 +793,11 @@
     hg_start(1, 0)
     hg_start(1, 1)
 
-    first = s * rows
-    row_at = lax.broadcasted_iota(jnp.int32, (rows, 128), 0)
-    lane_at = lax.broadcasted_iota(jnp.int32, (rows, rows), 1)
-    square = lax.broadcasted_iota(jnp.int32, (local, local), 0)
-    square_lane = lax.broadcasted_iota(jnp.int32, (local, local), 1)
-    same_head = (square // DH) == (square_lane // DH)
-    diagonal = square == square_lane
-    lane_head = lax.broadcasted_iota(jnp.int32, (rows, local), 1) // DH
-    before_thr, after_thr = [], []
-
-    def wide(value):
-        return jnp.concatenate([value] * (local // 128), axis=1)
-
-    def begin(offsets, place):
-        value = 0
-        for off in offsets:
-            value = jnp.where(off <= place, off, value)
-        return value
-
-    def through(offsets, which):
-        return jnp.where(
-            begin(offsets, which * rows + rows - 1) < which * rows, 1.0, 0.0
-        ).astype(F32)
-
-    def crops(b):
-        offsets, running = [], 0
-        for i in range(r.lengths.shape[1]):
-            offsets.append(running)
-            running = running + r.lengths[b, i]
-        start = jnp.zeros((rows, 128), jnp.int32)
-        for off in offsets:
-            start = jnp.where(off <= row_at + first, off, start)
-        last = begin(offsets, first + rows - 1)
-        r.mask[b] = jnp.where(
-            (lane_at + first >= wide(start)) & (lane_at <= wide(row_at)), 1.0, 0.0
-        ).astype(F32)
-        r.car[b] = jnp.where(start < first, 1.0, 0.0).astype(F32)
-        r.tail[b] = jnp.where(start == last, 1.0, 0.0).astype(F32)
-        before_thr.append(through(offsets, lax.rem(s + n - 1, n)))
-        after_thr.append(through(offsets, lax.rem(s + 1, n)))
-        keep = r.pixel[b : b + 1, :].astype(F32)
-        r.pmc[b] = dot_nn(
-            jnp.where(diagonal, keep, 0.0).astype(BF), jnp.ones((rows, 128), BF)
-        )
-
     def ag_step(j):
         ag_pass(SMALL, j)
         ag_pass(QKV, j)
         ag_pass(OUT, j)
 
-    crops(0)
     hg_forward(0, 0)
     ag_step(0)
     hg_forward(0, 1)

time: 136 us -> 136 us (level)
  no operation moved by 1% of the time
where the time goes in v7:
time: 136 us
  Pallas kernels  135 us (99%)
    pallas_call x1, Pallas kernels, on_each(): pl.pallas_call(functools.partial(body, n, m, ins + outs + list(vm) + list...  133 us

profile of v7, /device:TPU:0, one launch (start us, length us, event | category | flops | bytes accessed | tf_op | source)
XLA Modules:
  0.0 135.8 jit_solution(5141737526937512140)
XLA Ops:
  0.6 133.4 %layer.1 = (f32[2,256,256]{2,1,0:T(8,128)S(1)}, f32[2,256,256]{2,1,0:T(8,128)S(1)}, f32[3,128,256]{2,1,0:T(8,128)S(1)}, f32[128,256]{1,0:T(8,128)S(1)}, f32[128,...) custom-call(bf16[2,256,256]{2,1,0:T(8,128)(2,1)} %refs_0_.1, ...), custom_call_target="tpu_custom_call" | custom-call | tf_op jit(solution)/shard_map/layer/pallas_call | solution.py:1303
  134.1 1.6 %settle.1 = (f32[2,256,256]{2,1,0:T(8,128)}, f32[2,256,256]{2,1,0:T(8,128)}, f32[3,128,256]{2,1,0:T(8,128)}, f32[128,256]{1,0:T(8,128)}, f32[128,1024]{1,0:T(8,1...) custom-call(f32[2,256,256]{2,1,0:T(8,128)S(1)} %get-tuple-element.27.refs_0_, ...), custom_call_target="tpu_custom_call" | custom-call | tf_op jit(solution)/shard_map/settle/pallas_call | solution.py:1337

commit v8 on v7

--- a/solution.py
+++ b/solution.py
@@ -1073,6 +1073,13 @@
     hr_first(1, 0, pick(r.activ), product_nt(r.wd))
     hr_first(1, 1, pick(r.activ), product_nt(r.wd))
     rs_round(DOWN, 3)
+    r.upb[...] = jnp.zeros_like(r.upb)
+
+    def column_sums(i):
+        r.upb[...] += jnp.sum(r.g_hid[ds(i * tile, tile), :].astype(F32), axis=0, keepdims=True)
+
+    loop(tokens // tile, column_sums)
+
     for c in (0, 1):
         hg_forward(3, c)
     for c in (0, 1):
@@ -1210,12 +1217,6 @@
         remote(
             r.hs_send, r.hs_recv.at[h], r.hs_s.at[0], r.hs_r.at[0], s, lax.rem(h + i, m)
         ).start()
-    r.upb[...] = jnp.zeros_like(r.upb)
-
-    def column_sums(i):
-        r.upb[...] += jnp.sum(r.g_hid[ds(i * tile, tile), :].astype(F32), axis=0, keepdims=True)
-
-    loop(tokens // tile, column_sums)
     rs_round(OUT, 3)
     rs_round(QUERY, 3)
     rs_final(DOWN)

time: 136 us -> 136 us (level)
  no operation moved by 1% of the time
where the time goes in v8:
time: 136 us
  Pallas kernels  135 us (99%)
    pallas_call x1, Pallas kernels, on_each(): pl.pallas_call(functools.partial(body, n, m, ins + outs + list(vm) + list...  133 us

profile of v8, /device:TPU:0, one launch (start us, length us, event | category | flops | bytes accessed | tf_op | source)
XLA Modules:
  0.0 135.8 jit_solution(2737426719900772788)
XLA Ops:
  0.6 133.4 %layer.1 = (f32[2,256,256]{2,1,0:T(8,128)S(1)}, f32[2,256,256]{2,1,0:T(8,128)S(1)}, f32[3,128,256]{2,1,0:T(8,128)S(1)}, f32[128,256]{1,0:T(8,128)S(1)}, f32[128,...) custom-call(bf16[2,256,256]{2,1,0:T(8,128)(2,1)} %refs_0_.1, ...), custom_call_target="tpu_custom_call" | custom-call | tf_op jit(solution)/shard_map/layer/pallas_call | solution.py:1304
  134.1 1.6 %settle.1 = (f32[2,256,256]{2,1,0:T(8,128)}, f32[2,256,256]{2,1,0:T(8,128)}, f32[3,128,256]{2,1,0:T(8,128)}, f32[128,256]{1,0:T(8,128)}, f32[128,1024]{1,0:T(8,1...) custom-call(f32[2,256,256]{2,1,0:T(8,128)S(1)} %get-tuple-element.27.refs_0_, ...), custom_call_target="tpu_custom_call" | custom-call | tf_op jit(solution)/shard_map/settle/pallas_call | solution.py:1338
